TPU v7x, 32 devices: a whole 2x2x4 slice. The times are simulated.
32 devices in a mesh: lon: 8 (over y, x, core), lat: 4 (over z).
Axes of the slice: x: 2, y: 2, z: 4, core: 2. Of those that a mesh axis runs over, the one named last changes fastest.
Arguments:
- ensemble: float32 [8, 4, 80, 32, 256], P('lon', 'lat'), may hold values from -6 to 6
- obs_block: int32 [3, 128], replicated, may hold values from 0 to 31, as said below
- obs_column: int32 [3, 128], replicated, may hold values from 0 to 255
- obs_value: float32 [3, 128], replicated, may hold values from -8 to 8
- obs_error: float32 [3, 128], replicated, may hold values from 0.5 to 2
- loc_mask: int32 [8, 4, 3, 128, 256], P('lon', 'lat'), may hold values from 0 to 1, as said below
Outputs:
- analysis: float32 [8, 4, 80, 32, 256], P('lon', 'lat')
Inputs may be any that keep to these rules, and one draw needn't show every extreme that they name: `obs_block`: observations fall more often on blocks of low index. `loc_mask`: an observation may update only columns of its own block and of blocks at most two blocks away along longitude (cyclically) and latitude; all other blocks have zeros for it.
All inputs are finite; a program needn't handle non-finite values.
Results may differ from a plain program's by a relative error of at most 0.0001.
Values sent between devices are 32-bit elements; how exact they have to be, the bound alone decides.
No kernel may reach another device: no remote copies, remote signals or barrier semaphores. Data moves between devices by JAX's collectives and lax.ppermute only.
A program may use at most 64 MiB of HBM per device.

v0:
```python
import jax
import jax.numpy as jnp
from jax import lax
from jax.sharding import PartitionSpec as P


def solve_rows(whitened, innov_raw):
    count = whitened.shape[0]
    cmat = jnp.eye(count, dtype=jnp.float32) + jnp.dot(
        whitened, whitened.T, precision=lax.Precision.HIGHEST
    )
    chol = jnp.linalg.cholesky(cmat)
    gain_rows = jax.scipy.linalg.cho_solve((chol, True), whitened)
    innov = jax.scipy.linalg.cho_solve((chol, True), innov_raw)
    return (gain_rows, innov)


def body(ensemble, obs_block, obs_column, obs_value, obs_error, loc_mask):
    members = ensemble.shape[2]
    levels = ensemble.shape[3]
    columns = ensemble.shape[4]
    count = obs_block.shape[1]
    scale = 1.0 / jnp.sqrt(jnp.float32(members - 1))
    n_lat = lax.axis_size("lat")
    lat_here = lax.axis_index("lat")
    state = ensemble.reshape(members, levels * columns)
    col_ids = jnp.arange(columns, dtype=jnp.int32)
    for batch in range(obs_block.shape[0]):
        blocks = obs_block[batch]
        pick = obs_column[batch][:, None] == col_ids[None, :]
        surface = state[:, :columns]
        piece = lax.all_gather(surface[None], "lon", axis=0, tiled=True)
        width = piece.shape[0]
        ids = jnp.arange(width, dtype=jnp.int32) * n_lat + lat_here
        select = ((blocks[:, None] == ids[None, :])[:, :, None] & pick[:, None, :]).astype(
            jnp.float32
        )
        row_part = jnp.zeros((count, members), jnp.float32) + jnp.einsum(
            "pkc,kmc->pm", select, piece, precision=lax.Precision.HIGHEST
        )
        obs_ens = lax.psum(row_part, "lat")
        obs_mean = jnp.mean(obs_ens, axis=1)
        errors = obs_error[batch]
        whitened = (obs_ens - obs_mean[:, None]) * scale / errors[:, None]
        innov_raw = (obs_value[batch] - obs_mean) / errors
        gain_rows, innov = solve_rows(whitened, innov_raw)
        coef = jnp.concatenate([-0.5 * gain_rows.T, (innov * scale)[None, :]], axis=0)
        weights = loc_mask[0, 0, batch].astype(jnp.float32)
        mean = jnp.mean(state, axis=0)
        pert = state - mean[None, :]
        proj = jnp.dot(whitened, pert, precision=lax.Precision.HIGHEST)
        proj = (proj.reshape(count, levels, columns) * weights[:, None, :]).reshape(
            count, levels * columns
        )
        incr = jnp.dot(coef, proj, precision=lax.Precision.HIGHEST)
        state = pert + incr[:members] + (mean + incr[members])[None, :]
    return state.reshape(ensemble.shape)


def solution(mesh):
    placed = (
        P("lon", "lat", None, None, None),
        P(),
        P(),
        P(),
        P(),
        P("lon", "lat", None, None, None),
    )
    return jax.shard_map(
        body,
        mesh=mesh,
        in_specs=placed,
        out_specs=P("lon", "lat", None, None, None),
        check_vma=False,
    )
```

profile of v0, /device:TPU:0, one launch (start us, length us, event | category | flops | bytes accessed | tf_op | source)
XLA Modules:
  0.0 211.7 jit_solution(10639633567476785206)
XLA Ops:
  0.0 0.8 slice_bitcast_fusion.2
  0.9 3.4 %copy.32 = f32[10,8,32,256]{3,1,2,0:T(8,128)S(1)} copy(f32[10,8,32,256]{3,2,1,0:T(8,128)} %bitcast.215) | data formatting | bytes 5242880
  4.3 11.6 %all-gather = f32[640,256]{1,0:T(8,128)S(1)} all-gather(f32[80,256]{1,0:T(8,128)S(1)} %slice.116), channel_id=2, replica_groups=mesh['lon'=8,'lat'=4] {'lon'}, dimensions={0}, use_global_device_ids=true | all-gather | bytes 737280 | tf_op jit(solution)/shard_map/all_gather | solution.py:32
  16.0 0.7 convolution_bitcast_fusion.2
  16.8 20.2 %psum.21 = f32[128,80]{0,1:T(8,128)S(1)} all-reduce(f32[128,80]{0,1:T(8,128)S(1)} %convolution_bitcast_fusion.2), channel_id=1, replica_groups=mesh['lon'=8,'lat'=4] {'lat'}, use_global_device_ids=true, to_apply=%region_1.0 | all-reduce | flops 10240 | bytes 81920 | tf_op jit(solution)/shard_map/psum | solution.py:41
  37.0 0.3 convolution_add_fusion.2
  37.4 11.7 %cholesky.59 = f32[128,128]{1,0:T(8,128)S(1)} custom-call(f32[128,128]{1,0:T(8,128)S(1)} %fusion.63), custom_call_target="Cholesky" | custom-call | tf_op jit(solution)/shard_map/jit(cholesky)/cholesky | solution.py:12
  49.2 0.6 compare_reduce_fusion.2
  49.8 0.7 fusion.31
  50.5 9.8 %custom-call.16 = f32[1,128,128]{1,2,0:T(8,128)S(1)} custom-call(f32[1,128,128]{2,1,0:T(8,128)S(1)} %fusion.31), custom_call_target="InvertDiagBlocksLowerTriangular" | custom-call | tf_op jit(solution)/shard_map/jit(_cho_solve)/triangular_solve | solution.py:13
  60.3 0.3 fusion.61
  61.3 1.9 reduce_sum.54
  63.3 0.3 broadcast_subtract_fusion
  63.6 0.7 copy-done.2
  64.3 5.1 %fusion.8 = f32[128,32,256]{2,0,1:T(8,128)} fusion(f32[10,32,8,256]{3,2,1,0:T(8,128)S(1)} %bitcast.216, f32[128,256]{1,0:T(8,128)S(1)} %get-tuple-element.13, f32[128,80]{0,1:T(8,128)S(1)} %psum.21, f32[128]{0:T(128)S(1)} %get-tuple-element.18, f32[128]{0:T(128)S(1)} %broadcast_multiply_fusion.4), kind=kOutput, calls=%fused_computation.13 | convolution fusion | flops 1007712256 | bytes 6988800 | tf_op jit(solution)/shard_map/dot_general | solution.py:51
  69.5 5.6 %copy.21 = f32[128,32,256]{0,2,1:T(8,128)} copy(f32[128,32,256]{2,0,1:T(8,128)} %fusion.8) | data formatting | bytes 8388608 | tf_op jit(solution)/shard_map/mul | solution.py:52
  75.0 5.9 %fusion.34 = f32[81,8192]{1,0:T(8,128)S(1)} fusion(f32[128,8192]{0,1:T(8,128)} %bitcast.210, f32[1,128]{0,1:T(8,128)S(1)} %copy.19, f32[80,128]{0,1:T(8,128)S(1)} %fusion.15), kind=kOutput, calls=%fused_computation.62 | convolution fusion | flops 1019226240 | bytes 6889984 | tf_op jit(solution)/shard_map/dot_general | solution.py:55
  81.0 0.5 fusion.82
  81.5 1.5 copy-done
  83.0 10.1 %all-gather.1 = f32[640,256]{1,0:T(8,128)S(1)} all-gather(f32[80,256]{1,0:T(8,128)S(1)} %slice.119), channel_id=3, replica_groups=mesh['lon'=8,'lat'=4] {'lon'}, dimensions={0}, use_global_device_ids=true | all-gather | bytes 737280 | tf_op jit(solution)/shard_map/all_gather | solution.py:32
  93.2 0.7 convolution_bitcast_fusion.1
  93.9 16.3 %psum.22 = f32[128,80]{0,1:T(8,128)S(1)} all-reduce(f32[128,80]{0,1:T(8,128)S(1)} %convolution_bitcast_fusion.1), channel_id=1, replica_groups=mesh['lon'=8,'lat'=4] {'lat'}, use_global_device_ids=true, to_apply=%region_6.0 | all-reduce | flops 10240 | bytes 81920 | tf_op jit(solution)/shard_map/psum | solution.py:41
  110.2 0.3 convolution_add_fusion.1
  110.7 11.7 %cholesky.70 = f32[128,128]{1,0:T(8,128)S(1)} custom-call(f32[128,128]{1,0:T(8,128)S(1)} %fusion.57), custom_call_target="Cholesky" | custom-call | tf_op jit(solution)/shard_map/jit(cholesky)/cholesky | solution.py:12
  122.4 0.7 compare_reduce_fusion.1
  123.1 0.7 fusion.32
  123.8 9.8 %custom-call.18 = f32[1,128,128]{1,2,0:T(8,128)S(1)} custom-call(f32[1,128,128]{2,1,0:T(8,128)S(1)} %fusion.32), custom_call_target="InvertDiagBlocksLowerTriangular" | custom-call | tf_op jit(solution)/shard_map/jit(_cho_solve)/triangular_solve | solution.py:13
  133.6 0.3 fusion.55
  134.7 0.3 mul.86
  135.0 3.3 %copy.35 = f32[16,8,32,256]{3,1,2,0:T(8,128)S(1)} copy(f32[16,8,32,256]{3,2,1,0:T(8,128)S(1)} %bitcast.213) | data formatting | bytes 8388608
  138.4 3.8 %convolution_multiply_fusion.1 = f32[128,8192]{1,0:T(8,128)S(1)} fusion(f32[128,8192]{1,0:T(8,128)S(1)} %bitcast.211, f32[80,8192]{1,0:T(8,128)S(1)} %copy-done.1, f32[8192]{0:T(1024)S(1)} %broadcast_multiply_fusion.1, f32[128,80]{0,1:T(8,128)S(1)} %psum.22, f32[128]{0:T(128)S(1)} %get-tuple-element.19, f32[128]{0:T(128)S(1)} %broadcast_multiply_fusion.3), kind=kOutput, calls=%fused_computation.1 | convolution fusion | flops 1008367616 | bytes 11084800 | tf_op jit(solution)/shard_map/dot_general | solution.py:51
  142.1 3.0 %fusion.38 = f32[81,8192]{1,0:T(8,128)S(1)} fusion(f32[128,8192]{1,0:T(8,128)S(1)} %convolution_multiply_fusion.1, f32[1,128]{0,1:T(8,128)S(1)} %copy.24, f32[80,128]{0,1:T(8,128)S(1)} %fusion.14), kind=kOutput, calls=%fused_computation.66 | convolution fusion | flops 1019226240 | bytes 6889984 | tf_op jit(solution)/shard_map/dot_general | solution.py:55
  145.2 0.5 fusion.80
  145.7 9.1 %all-gather.2 = f32[640,256]{1,0:T(8,128)S(1)} all-gather(f32[80,256]{1,0:T(8,128)S(1)} %slice.122), channel_id=4, replica_groups=mesh['lon'=8,'lat'=4] {'lon'}, dimensions={0}, use_global_device_ids=true | all-gather | bytes 737280 | tf_op jit(solution)/shard_map/all_gather | solution.py:32
  155.0 0.7 convolution_bitcast_fusion
  155.7 18.4 %psum.23 = f32[128,80]{0,1:T(8,128)S(1)} all-reduce(f32[128,80]{0,1:T(8,128)S(1)} %convolution_bitcast_fusion), channel_id=1, replica_groups=mesh['lon'=8,'lat'=4] {'lat'}, use_global_device_ids=true, to_apply=%region_9.13 | all-reduce | flops 10240 | bytes 81920 | tf_op jit(solution)/shard_map/psum | solution.py:41
  174.1 0.3 convolution_add_fusion
  174.5 11.7 %cholesky.81 = f32[128,128]{1,0:T(8,128)S(1)} custom-call(f32[128,128]{1,0:T(8,128)S(1)} %fusion.51), custom_call_target="Cholesky" | custom-call | tf_op jit(solution)/shard_map/jit(cholesky)/cholesky | solution.py:12
  186.3 0.6 compare_reduce_fusion
  186.9 0.7 fusion.33
  187.6 9.8 %custom-call.20 = f32[1,128,128]{1,2,0:T(8,128)S(1)} custom-call(f32[1,128,128]{2,1,0:T(8,128)S(1)} %fusion.33), custom_call_target="InvertDiagBlocksLowerTriangular" | custom-call | tf_op jit(solution)/shard_map/jit(_cho_solve)/triangular_solve | solution.py:13
  197.4 0.3 fusion.49
  198.4 0.3 mul.93
  198.8 3.3 %copy.36 = f32[16,8,32,256]{3,1,2,0:T(8,128)S(1)} copy(f32[16,8,32,256]{3,2,1,0:T(8,128)S(1)} %bitcast.214) | data formatting | bytes 8388608
  202.1 3.7 %convolution_multiply_fusion = f32[128,8192]{1,0:T(8,128)S(1)} fusion(f32[128,8192]{1,0:T(8,128)S(1)} %bitcast.212, f32[80,8192]{1,0:T(8,128)S(1)} %get-tuple-element.8, f32[8192]{0:T(1024)S(1)} %broadcast_multiply_fusion, f32[128,80]{0,1:T(8,128)S(1)} %psum.23, f32[128]{0:T(128)S(1)} %get-tuple-element.17, f32[128]{0:T(128)S(1)} %broadcast_multiply_fusion.2), kind=kOutput, calls=%fused_computation | convolution fusion | flops 1008367616 | bytes 11084800 | tf_op jit(solution)/shard_map/dot_general | solution.py:51
  205.8 3.0 %fusion.42 = f32[81,8192]{1,0:T(8,128)S(1)} fusion(f32[128,8192]{1,0:T(8,128)S(1)} %convolution_multiply_fusion, f32[1,128]{0,1:T(8,128)S(1)} %copy.27, f32[80,128]{0,1:T(8,128)S(1)} %fusion.13), kind=kOutput, calls=%fused_computation.70 | convolution fusion | flops 1019226240 | bytes 6889984 | tf_op jit(solution)/shard_map/dot_general | solution.py:55
  208.9 0.3 fusion.3
  209.2 2.3 %copy.37 = f32[10,8,32,256]{3,2,1,0:T(8,128)} copy(f32[10,8,32,256]{3,1,2,0:T(8,128)S(1)} %bitcast.217) | data formatting | bytes 5242880
  (56 shorter events, 3.2 us)
Async XLA Ops:
  0.9 15.1 %copy-start.5 = (s32[3,128]{1,0:T(4,128)S(1)}, s32[3,128]{1,0:T(4,128)}, u32[]{:S(2)}) copy-start(s32[3,128]{1,0:T(4,128)} %param.13) | copy-start | bytes 4612
  0.9 36.1 %copy-start.3 = (f32[3,128]{1,0:T(4,128)S(1)}, f32[3,128]{1,0:T(4,128)}, u32[]{:S(2)}) copy-start(f32[3,128]{1,0:T(4,128)} %param.15) | copy-start | bytes 4612
  4.3 56.5 %copy-start.4 = (f32[3,128]{1,0:T(4,128)S(1)}, f32[3,128]{1,0:T(4,128)}, u32[]{:S(2)}) copy-start(f32[3,128]{1,0:T(4,128)} %param.14) | copy-start | bytes 4612
  63.3 1.0 copy-start.2
  81.5 1.5 copy-start
  135.0 3.4 %copy-start.1 = (f32[80,8192]{1,0:T(8,128)S(1)}, f32[80,8192]{1,0:T(8,128)}, u32[]{:S(2)}) copy-start(f32[80,8192]{1,0:T(8,128)} %copy-done) | copy-start | bytes 7864324
where the time goes:
time: 215 us; the launch traced here: 212 us
  blocking collectives  85.7 us (40%)
  other arithmetic  72.7 us (34%)
  matrix products  30.2 us (14%)
  local copies, waits for them, and re-layouts  22.4 us (10%)
    psum x3, blocking collectives, body(): obs_ens = lax.psum(row_part, 'lat')  54.8 us
    another operation x9, other arithmetic, solve_rows(): chol = jnp.linalg.cholesky(cmat)  37.2 us
    another operation x6, other arithmetic, solve_rows(): gain_rows = jax.scipy.linalg.cho_solve((chol, True), whitened)  31.4 us
    all_gather x3, blocking collectives, body(): piece = lax.all_gather(surface[None], 'lon', axis=0, tiled=True)  30.8 us
    unnamed x18, local copies, waits for them, and re-layouts  14.6 us
    dot_general x3, matrix products, body(): proj = jnp.dot(whitened, pert, precision=lax.Precision.HIGHEST)  12.6 us
    dot_general x3, matrix products, body(): incr = jnp.dot(coef, proj, precision=lax.Precision.HIGHEST)  12 us
    mul x3, local copies, waits for them, and re-layouts, body(): proj.reshape(count, levels, columns) * weights[:, None, :]  6.22 us

commit v1 on v0

v1 whole, which is shorter than its diff:
```python
import functools
import jax
import jax.numpy as jnp
from jax import lax
from jax.experimental import pallas as pl
from jax.experimental.pallas import tpu as pltpu
from jax.sharding import PartitionSpec as P

F32 = jnp.float32
BF16 = jnp.bfloat16
HIGHEST = lax.Precision.HIGHEST
DOUBLINGS = 6
ENOUGH = 2.0**25
VMEM_LIMIT = 48 * 1024 * 1024


def mm(a, b, contract=((1,), (0,)), precision=HIGHEST):
    return lax.dot_general(
        a, b, (contract, ((), ())), precision=precision, preferred_element_type=F32
    )


def split(x):
    hi = x.astype(BF16)
    return hi, (x - hi.astype(F32)).astype(BF16)


def pick_kernel(n_lat, batches, block_ref, column_ref, mask_ref, *refs):
    ens_refs, out_ref = refs[:-1], refs[-1]
    members, rows, lanes = ens_refs[0].shape
    columns = mask_ref.shape[2]
    count = block_ref.shape[1]
    here = lax.axis_index("lon") * n_lat + lax.axis_index("lat")
    ids = lax.broadcasted_iota(jnp.int32, (columns, count), 0)
    picks = []
    for b in range(batches):
        key = jnp.where(block_ref[b : b + 1] == here, column_ref[b : b + 1], -1)
        picks.append((ids == key).astype(F32).astype(BF16))
    surface = jnp.concatenate(
        [ref.reshape(members * rows, lanes)[pl.ds(0, members, stride=rows), :] for ref in ens_refs],
        axis=1,
    )
    hi = surface.astype(BF16)
    rest = surface - hi.astype(F32)
    mid = rest.astype(BF16)
    low = (rest - mid.astype(F32)).astype(BF16)
    at = 0
    for b in range(batches):
        parts = [mm(part, picks[b], precision=None) for part in (hi, mid, low)]
        out_ref[at : at + members, :] = (parts[2] + parts[1]) + parts[0]
        at += members
    for b in range(batches - 1):
        entries = mask_ref[b].astype(F32).astype(BF16)
        for later in range(b + 1, batches):
            out_ref[at : at + count, :] = mm(entries, picks[later], precision=None)
            at += count
    if at < out_ref.shape[0]:
        out_ref[at:, :] = jnp.zeros((out_ref.shape[0] - at, count), F32)


def bounds(gram):
    norm = jnp.sum(jnp.sum(gram * gram, axis=0, keepdims=True), axis=1, keepdims=True)
    return 1.0 + jnp.maximum(jnp.sqrt(norm) * 1.0001, 0.25)


def solve(w, eye):
    gram = mm(w, w, ((1,), (1,)))
    gram2 = mm(gram, gram)
    gw = mm(gram, w)
    top = bounds(gram)
    alpha = 2.0 / (top + 1.0)
    beta = 1.0 - alpha
    t = (top + 1.0) / (top - 1.0)
    t = 2.0 * t * t - 1.0
    d = 1.0 / t
    v = (1.0 + d) * alpha * (w + (beta * w - alpha * gw))
    e = (1.0 + d) * (
        (beta * beta) * eye - (2.0 * alpha * beta) * gram + (alpha * alpha) * gram2
    ) - d * eye
    for step in range(1, DOUBLINGS):
        t = jnp.minimum(2.0 * t * t - 1.0, 1e15)
        d = 1.0 / t
        v = (1.0 + d) * (v + mm(e, v))
        if step < DOUBLINGS - 1:
            e = (1.0 + d) * mm(e, e) - d * eye
    return v, t


def solve_long(w, eye):
    gram = mm(w, w, ((1,), (1,)))
    top = bounds(gram)
    alpha = 2.0 / (top + 1.0)

    def more(carry):
        return carry[2][0, 0] < ENOUGH

    def double(carry):
        e, x, t = carry
        t = jnp.minimum(2.0 * t * t - 1.0, 1e15)
        d = 1.0 / t
        return (1.0 + d) * mm(e, e) - d * eye, (1.0 + d) * (x + mm(e, x)), t

    e = (1.0 - alpha) * eye - alpha * gram
    x = alpha * eye
    x = lax.while_loop(more, double, (e, x, (top + 1.0) / (top - 1.0)))[1]

    def correct(_, v):
        return v + mm(x, w - (v + mm(gram, v)))

    return lax.fori_loop(0, 3, correct, mm(x, w))


def assimilate_kernel(
    batches, members, rows_ref, value_ref, error_ref, mask_ref, ens_ref, out_ref,
    state, result, wide, coef, in_sem, out_sem,
):
    count = rows_ref.shape[1]
    chunks, halves, _, sub, lanes = state.shape

    def piece(ref, j, h):
        return ref.at[:, j, :, h * lanes : (h + 1) * lanes]

    loads = [
        pltpu.make_async_copy(piece(ens_ref, j, h), state.at[j, h], in_sem.at[j, h])
        for j in range(chunks)
        for h in range(halves)
    ]
    for load in loads:
        load.start()
    scale = 1.0 / jnp.sqrt(jnp.full((1, 1), members - 1, F32))
    eye = (
        lax.broadcasted_iota(jnp.int32, (members, members), 0)
        == lax.broadcasted_iota(jnp.int32, (members, members), 1)
    ).astype(F32)
    def analyse(solver):
        lows = []
        obs = [rows_ref[b * members : (b + 1) * members, :] for b in range(batches)]
        at = batches * members
        for b in range(batches):
            mean = jnp.mean(obs[b], axis=0, keepdims=True)
            errors = error_ref[b : b + 1]
            w = (obs[b] - mean) * scale / errors
            raw = (value_ref[b : b + 1] - mean) / errors
            along = jnp.sum(w * raw, axis=1, keepdims=True)
            projected = []
            for later in range(b + 1, batches):
                projected.append(rows_ref[at : at + count, :] * mm(w, obs[later], ((0,), (0,))))
                at += count
            v, t = solver(w, eye)
            lows.append(t)
            innov = raw - jnp.sum(v * along, axis=0, keepdims=True)
            change = -0.5 * v + scale * innov
            for later in range(b + 1, batches):
                obs[later] = obs[later] + mm(change, projected[later - b - 1])
            hi = w.astype(BF16).astype(F32)
            spare = jnp.zeros((wide.shape[2] - 3 * members, count), F32)
            stack = jnp.concatenate([hi, w - hi, hi, spare], axis=0)
            wide[b] = stack.T.astype(BF16)
            hi, low = split(change)
            coef[b] = jnp.concatenate([hi, hi, low], axis=1)
        return functools.reduce(jnp.minimum, lows)

    reached = analyse(solve)

    @pl.when(jnp.logical_not(reached[0, 0] >= ENOUGH))
    def _():
        analyse(lambda w, eye: (solve_long(w, eye), jnp.ones((1, 1), F32)))

    stores = [
        pltpu.make_async_copy(result.at[j, h], piece(out_ref, j, h), out_sem.at[j, h])
        for j in range(chunks)
        for h in range(halves)
    ]
    for j in range(chunks):
        src, dst = [], []
        for h in range(halves):
            loads[j * halves + h].wait()
            src.append(state.at[j, h].reshape(members * sub, lanes))
            dst.append(result.at[j, h].reshape(members * sub, lanes))
        for level in range(sub):
            cells = jnp.concatenate([r[pl.ds(level, members, stride=sub), :] for r in src], axis=1)
            for b in range(batches):
                hi, low = split(cells)
                stack = jnp.concatenate([hi, hi, low], axis=0)
                proj = mm(wide[b][:, : 3 * members], stack, precision=None)
                proj = proj * mask_ref[b].astype(F32)
                hi, low = split(proj)
                stack = jnp.concatenate([hi, low, hi], axis=0)
                cells = cells + mm(coef[b], stack, precision=None)
            for h in range(halves):
                dst[h][pl.ds(level, members, stride=sub), :] = cells[:, h * lanes : (h + 1) * lanes]
        for h in range(halves):
            stores[j * halves + h].start()
    for store in stores:
        store.wait()


def exchange(x):
    n_lon = lax.axis_size("lon")
    n_lat = lax.axis_size("lat")
    parts = x.reshape(n_lon, x.shape[0] // n_lon, x.shape[1])
    y = lax.all_to_all(parts, "lon", 0, 0, tiled=True).sum(0)
    if n_lat & (n_lat - 1) == 0:
        k = 1
        while k < n_lat:
            y = y + lax.ppermute(y, "lat", [(i, i ^ k) for i in range(n_lat)])
            k *= 2
    else:
        y = lax.psum(y, "lat")
    return lax.all_gather(y, "lon", axis=0, tiled=True)


def body(ensemble, obs_block, obs_column, obs_value, obs_error, loc_mask):
    members, levels, columns = ensemble.shape[2:]
    batches, count = obs_block.shape
    n_lon = lax.axis_size("lon")
    n_lat = lax.axis_size("lat")
    sub, lanes = 8, 128
    halves = columns // lanes
    chunks = levels // sub
    field = ensemble.reshape(members, levels, columns)
    masks = loc_mask.reshape(batches, count, columns)
    used = batches * members + batches * (batches - 1) // 2 * count
    total = -(-used // (8 * n_lon)) * 8 * n_lon
    vmem = pl.BlockSpec(memory_space=pltpu.VMEM)
    packed = pl.pallas_call(
        functools.partial(pick_kernel, n_lat, batches),
        grid=(1,),
        out_shape=jax.ShapeDtypeStruct((total, count), F32),
        in_specs=[
            pl.BlockSpec((batches, count), lambda i: (0, 0)),
            pl.BlockSpec((batches, count), lambda i: (0, 0)),
            pl.BlockSpec((batches - 1, count, columns), lambda i: (0, 0, 0)),
        ]
        + [
            pl.BlockSpec((members, sub, lanes), functools.partial(lambda h, i: (0, 0, h), h))
            for h in range(halves)
        ],
        out_specs=pl.BlockSpec((total, count), lambda i: (0, 0)),
        compiler_params=pltpu.CompilerParams(vmem_limit_bytes=VMEM_LIMIT),
        name="pick",
    )(obs_block, obs_column, masks, *[field] * halves)
    rows = exchange(packed)
    result = pl.pallas_call(
        functools.partial(assimilate_kernel, batches, members),
        out_shape=jax.ShapeDtypeStruct((members, chunks, sub, columns), F32),
        in_specs=[vmem, vmem, vmem, vmem, pl.BlockSpec(memory_space=pl.ANY)],
        out_specs=pl.BlockSpec(memory_space=pl.ANY),
        scratch_shapes=[
            pltpu.VMEM((chunks, halves, members, sub, lanes), F32),
            pltpu.VMEM((chunks, halves, members, sub, lanes), F32),
            pltpu.VMEM((batches, count, -(-3 * members // 128) * 128), BF16),
            pltpu.VMEM((batches, members, 3 * count), BF16),
            pltpu.SemaphoreType.DMA((chunks, halves)),
            pltpu.SemaphoreType.DMA((chunks, halves)),
        ],
        compiler_params=pltpu.CompilerParams(vmem_limit_bytes=VMEM_LIMIT),
        name="assimilate",
    )(rows, obs_value, obs_error, masks, field.reshape(members, chunks, sub, columns))
    return result.reshape(ensemble.shape)


def solution(mesh):
    placed = (
        P("lon", "lat", None, None, None),
        P(),
        P(),
        P(),
        P(),
        P("lon", "lat", None, None, None),
    )
    return jax.shard_map(
        body,
        mesh=mesh,
        in_specs=placed,
        out_specs=P("lon", "lat", None, None, None),
        check_vma=False,
    )
```

time: 215 us -> 62.2 us (0.29); the launches traced: 212 us -> 61.9 us
  other arithmetic: 72.7 us -> 0.03 us
  blocking collectives: 85.7 us -> 21.2 us
  matrix products: 30.2 us -> 0 us
  Pallas kernels: 0 us -> 27.4 us
  local copies, waits for them, and re-layouts: 22.4 us -> 4.11 us
  waiting for transfers between devices: 0 us -> 4.74 us
  starting transfers between devices: 0 us -> 4.23 us
    another operation x15 -> x0, other arithmetic: 68.7 us -> none  [the longest x9 37.2 us: solve_rows(): chol = jnp.linalg.cholesky(cmat)]
    psum x3 -> x0, blocking collectives: 54.8 us -> none  [body(): obs_ens = lax.psum(row_part, 'lat')]
    dot_general x12 -> x0, matrix products: 27.7 us -> none  [the longest x3 12.6 us: body(): proj = jnp.dot(whitened, pert, precision=lax.Precision.HIGHEST)]
    pallas_call x0 -> x2, Pallas kernels: none -> 27.4 us  [the longest x1 27 us: body(): pl.pallas_call(functools.partial(assimilate_kernel, batches, members), ou...]
    all_gather x3 -> x1, blocking collectives: 30.8 us -> 8.48 us  [exchange(): return lax.all_gather(y, 'lon', axis=0, tiled=True)]
    all_to_all x0 -> x1, blocking collectives: none -> 12.7 us  [exchange(): y = lax.all_to_all(parts, 'lon', 0, 0, tiled=True).sum(0)]
    unnamed x18 -> x16, local copies, waits for them, and re-layouts: 14.6 us -> 4.11 us
    mul x3 -> x0, local copies, waits for them, and re-layouts: 6.22 us -> none  [body(): proj.reshape(count, levels, columns) * weights[:, None, :]]
  transfers between devices with their start and end apart: 0 -> 2, of which waited for: 0 -> 2; matrix products, arithmetic and copies ran while one was open for 0% -> 0% of each run, Pallas kernels for 0% -> 0%
where the time goes in v1:
time: 62.2 us; the launch traced here: 61.9 us
  Pallas kernels  27.4 us (44%)
  blocking collectives  21.2 us (34%)
  waiting for transfers between devices  4.74 us (8%)
  starting transfers between devices  4.23 us (7%)
  local copies, waits for them, and re-layouts  4.11 us (7%)
    pallas_call x1, Pallas kernels, body(): pl.pallas_call(functools.partial(assimilate_kernel, batches, members), ou...  27 us
    all_to_all x1, blocking collectives, exchange(): y = lax.all_to_all(parts, 'lon', 0, 0, tiled=True).sum(0)  12.7 us
    all_gather x1, blocking collectives, exchange(): return lax.all_gather(y, 'lon', axis=0, tiled=True)  8.48 us
    ppermute x2, waiting for transfers between devices, exchange(): y = y + lax.ppermute(y, 'lat', [(i, i ^ k) for i in range(n_lat)])  4.74 us
    ppermute x2, starting transfers between devices, exchange(): y = y + lax.ppermute(y, 'lat', [(i, i ^ k) for i in range(n_lat)])  4.23 us
    unnamed x16, local copies, waits for them, and re-layouts  4.11 us
  transfers between devices with their start and end apart: 2, of which 2 were waited for; matrix products, arithmetic and copies ran while one was open for 0% of the time, Pallas kernels for 0%

profile of v1, /device:TPU:0, one launch (start us, length us, event | category | flops | bytes accessed | tf_op | source)
XLA Modules:
  0.0 61.9 jit_solution(18075954446770578933)
XLA Ops:
  0.0 0.0 copy-start
  0.0 1.7 %copy-done = f32[1,1,80,32,256]{4,3,2,1,0:T(8,128)S(1)} copy-done((f32[1,1,80,32,256]{4,3,2,1,0:T(8,128)S(1)}, f32[1,1,80,32,256]{4,3,2,1,0:T(8,128)}, u32[]{:S(2)}) %copy-start) | copy-done | bytes 2621464
  1.7 0.0 copy-start.2
  1.7 1.0 %copy-done.2 = s32[1,1,3,128,256]{4,3,2,1,0:T(8,128)S(1)} copy-done((s32[1,1,3,128,256]{4,3,2,1,0:T(8,128)S(1)}, s32[1,1,3,128,256]{4,3,2,1,0:T(8,128)}, u32[]{:S(2)}) %copy-start.2) | copy-done | bytes 393240
  2.7 0.0 copy-start.4
  2.7 0.7 %copy-done.4 = s32[3,128]{1,0:T(4,128)S(1)} copy-done((s32[3,128]{1,0:T(4,128)S(1)}, s32[3,128]{1,0:T(4,128)}, u32[]{:S(2)}) %copy-start.4) | copy-done | bytes 1560
  3.4 0.0 copy-start.5
  3.4 0.7 %copy-done.5 = s32[3,128]{1,0:T(4,128)S(1)} copy-done((s32[3,128]{1,0:T(4,128)S(1)}, s32[3,128]{1,0:T(4,128)}, u32[]{:S(2)}) %copy-start.5) | copy-done | bytes 1560
  4.1 0.0 copy-start.1
  4.1 0.0 copy-start.3
  4.1 0.0 copy-start.6
  4.1 0.0 copy-start.7
  4.1 0.3 pick.1
  4.5 12.7 %all_to_all.5 = f32[8,80,128]{2,1,0:T(8,128)S(1)} all-to-all(f32[8,80,128]{2,1,0:T(8,128)S(1)} %bitcast.10), channel_id=1, replica_groups=mesh['lon'=8,'lat'=4] {'lon'}, dimensions={0} | all-to-all | bytes 655360 | tf_op jit(solution)/shard_map/all_to_all | solution.py:202
  17.2 1.6 %collective-permute-start = (f32[80,128]{1,0:T(8,128)S(1)}, f32[80,128]{1,0:T(8,128)S(1)}, u32[]{:S(2)}, u32[]{:S(2)}) collective-permute-start(f32[80,128]{1,0:T(8,128)S(1)} %reduce_sum.9), channel_id=1, source_target_pairs={{0,1},{1,0},{2,3},{3,2},{4,5},{5,4},{6,7},{7,6},{8,9},{9,8},{10,11... | collective-permute-start | bytes 122888 | tf_op jit(solution)/shard_map/ppermute | solution.py:206
  18.9 2.4 %collective-permute-done = f32[80,128]{1,0:T(8,128)S(1)} collective-permute-done((f32[80,128]{1,0:T(8,128)S(1)}, f32[80,128]{1,0:T(8,128)S(1)}, u32[]{:S(2)}, u32[]{:S(2)}) %collective-permute-start) | collective-permute-done | bytes 40992 | tf_op jit(solution)/shard_map/ppermute | solution.py:206
  21.3 2.6 %collective-permute-start.1 = (f32[80,128]{1,0:T(8,128)S(1)}, f32[80,128]{1,0:T(8,128)S(1)}, u32[]{:S(2)}, u32[]{:S(2)}) collective-permute-start(f32[80,128]{1,0:T(8,128)S(1)} %add.6), channel_id=1, source_target_pairs={{0,2},{1,3},{2,0},{3,1},{4,6},{5,7},{6,4},{7,5},{8,10},{9,11},{10,... | collective-permute-start | bytes 122888 | tf_op jit(solution)/shard_map/ppermute | solution.py:206
  23.9 2.3 %collective-permute-done.1 = f32[80,128]{1,0:T(8,128)S(1)} collective-permute-done((f32[80,128]{1,0:T(8,128)S(1)}, f32[80,128]{1,0:T(8,128)S(1)}, u32[]{:S(2)}, u32[]{:S(2)}) %collective-permute-start.1) | collective-permute-done | bytes 40992 | tf_op jit(solution)/shard_map/ppermute | solution.py:206
  26.2 8.5 %all_gather.3.rows_ref = f32[640,128]{1,0:T(8,128)S(1)} all-gather(f32[80,128]{1,0:T(8,128)S(1)} %add.7), channel_id=1, replica_groups=mesh['lon'=8,'lat'=4] {'lon'}, dimensions={0}, use_global_device_ids=true | all-gather | bytes 368640 | tf_op jit(solution)/shard_map/all_gather | solution.py:210
  34.7 0.0 copy-done.1
  34.7 0.0 copy-done.3
  34.7 0.0 copy-done.6
  34.7 0.0 copy-done.7
  34.7 27.0 %assimilate.1 = f32[80,4,8,256]{3,2,1,0:T(8,128)} custom-call(f32[640,128]{1,0:T(8,128)S(1)} %all_gather.3.rows_ref, f32[3,128]{1,0:T(4,128)S(1)} %copy-done.6, f32[3,128]{1,0:T(4,128)S(1)} %copy-done.7, s32[3,128,256]{2,1,0:T(8,128)S(1)} %bitcast.9, f32[80,4,8,256]{3,2,1,0:T(8,128)S(1)} %bitcast.7), custom_call_target="tpu_custom_call" | custom-call | tf_op jit(solution)/shard_map/assimilate/pallas_call | solution.py:244
  (3 shorter events, 0.0 us)
Async XLA Ops:
  0.0 1.7 %copy-start = (f32[1,1,80,32,256]{4,3,2,1,0:T(8,128)S(1)}, f32[1,1,80,32,256]{4,3,2,1,0:T(8,128)}, u32[]{:S(2)}) copy-start(f32[1,1,80,32,256]{4,3,2,1,0:T(8,128)} %param.6) | copy-start | bytes 7864324
  1.7 1.0 %copy-start.2 = (s32[1,1,3,128,256]{4,3,2,1,0:T(8,128)S(1)}, s32[1,1,3,128,256]{4,3,2,1,0:T(8,128)}, u32[]{:S(2)}) copy-start(s32[1,1,3,128,256]{4,3,2,1,0:T(8,128)} %param.11) | copy-start | bytes 1179652
  2.7 0.7 %copy-start.4 = (s32[3,128]{1,0:T(4,128)S(1)}, s32[3,128]{1,0:T(4,128)}, u32[]{:S(2)}) copy-start(s32[3,128]{1,0:T(4,128)} %block_ref.1) | copy-start | bytes 4612
  3.4 0.7 %copy-start.5 = (s32[3,128]{1,0:T(4,128)S(1)}, s32[3,128]{1,0:T(4,128)}, u32[]{:S(2)}) copy-start(s32[3,128]{1,0:T(4,128)} %column_ref.1) | copy-start | bytes 4612
  4.1 30.6 %copy-start.1 = (f32[1,1,80,32,256]{4,3,2,1,0:T(8,128)S(1)}, f32[1,1,80,32,256]{4,3,2,1,0:T(8,128)}, u32[]{:S(2)}) copy-start(f32[1,1,80,32,256]{4,3,2,1,0:T(8,128)} %param.6) | copy-start | bytes 7864324
  4.1 30.6 %copy-start.3 = (s32[1,1,3,128,256]{4,3,2,1,0:T(8,128)S(1)}, s32[1,1,3,128,256]{4,3,2,1,0:T(8,128)}, u32[]{:S(2)}) copy-start(s32[1,1,3,128,256]{4,3,2,1,0:T(8,128)} %param.11) | copy-start | bytes 1179652
  4.1 30.6 %copy-start.6 = (f32[3,128]{1,0:T(4,128)S(1)}, f32[3,128]{1,0:T(4,128)}, u32[]{:S(2)}) copy-start(f32[3,128]{1,0:T(4,128)} %value_ref.1) | copy-start | bytes 4612
  4.1 30.6 %copy-start.7 = (f32[3,128]{1,0:T(4,128)S(1)}, f32[3,128]{1,0:T(4,128)}, u32[]{:S(2)}) copy-start(f32[3,128]{1,0:T(4,128)} %error_ref.1) | copy-start | bytes 4612
  17.2 4.1 %collective-permute-start = (f32[80,128]{1,0:T(8,128)S(1)}, f32[80,128]{1,0:T(8,128)S(1)}, u32[]{:S(2)}, u32[]{:S(2)}) collective-permute-start(f32[80,128]{1,0:T(8,128)S(1)} %reduce_sum.9), channel_id=1, source_target_pairs={{0,1},{1,0},{2,3},{3,2},{4,5},{5,4},{6,7},{7,6},{8,9},{9,8},{10,11... | collective-permute-start | bytes 122888 | tf_op jit(solution)/shard_map/ppermute | solution.py:206
  21.3 4.9 %collective-permute-start.1 = (f32[80,128]{1,0:T(8,128)S(1)}, f32[80,128]{1,0:T(8,128)S(1)}, u32[]{:S(2)}, u32[]{:S(2)}) collective-permute-start(f32[80,128]{1,0:T(8,128)S(1)} %add.6), channel_id=1, source_target_pairs={{0,2},{1,3},{2,0},{3,1},{4,6},{5,7},{6,4},{7,5},{8,10},{9,11},{10,... | collective-permute-start | bytes 122888 | tf_op jit(solution)/shard_map/ppermute | solution.py:206

commit v2 on v1

--- a/solution.py
+++ b/solution.py
@@ -10,6 +10,7 @@
 BF16 = jnp.bfloat16
 HIGHEST = lax.Precision.HIGHEST
 DOUBLINGS = 6
+LEVELS_AT_ONCE = 8
 ENOUGH = 2.0**25
 VMEM_LIMIT = 48 * 1024 * 1024
 
@@ -25,21 +26,28 @@
     return hi, (x - hi.astype(F32)).astype(BF16)
 
 
-def pick_kernel(n_lat, batches, block_ref, column_ref, mask_ref, *refs):
-    ens_refs, out_ref = refs[:-1], refs[-1]
-    members, rows, lanes = ens_refs[0].shape
-    columns = mask_ref.shape[2]
-    count = block_ref.shape[1]
+def pick_kernel(n_lat, block_hbm, column_hbm, mask_hbm, ens_hbm, out_ref, block_ref, column_ref, mask_ref, surface_ref, sems):
+    batches, count = block_ref.shape
+    members, columns = surface_ref.shape
+    pairs = [
+        (block_hbm, block_ref),
+        (column_hbm, column_ref),
+        (ens_hbm.at[:, 0, :], surface_ref),
+        (mask_hbm.at[: batches - 1], mask_ref),
+    ]
+    copies = [pltpu.make_async_copy(a, b, sems.at[i]) for i, (a, b) in enumerate(pairs)]
+    for copy in copies:
+        copy.start()
     here = lax.axis_index("lon") * n_lat + lax.axis_index("lat")
     ids = lax.broadcasted_iota(jnp.int32, (columns, count), 0)
+    copies[0].wait()
+    copies[1].wait()
     picks = []
     for b in range(batches):
         key = jnp.where(block_ref[b : b + 1] == here, column_ref[b : b + 1], -1)
         picks.append((ids == key).astype(F32).astype(BF16))
-    surface = jnp.concatenate(
-        [ref.reshape(members * rows, lanes)[pl.ds(0, members, stride=rows), :] for ref in ens_refs],
-        axis=1,
-    )
+    copies[2].wait()
+    surface = surface_ref[...]
     hi = surface.astype(BF16)
     rest = surface - hi.astype(F32)
     mid = rest.astype(BF16)
@@ -49,6 +57,7 @@
         parts = [mm(part, picks[b], precision=None) for part in (hi, mid, low)]
         out_ref[at : at + members, :] = (parts[2] + parts[1]) + parts[0]
         at += members
+    copies[3].wait()
     for b in range(batches - 1):
         entries = mask_ref[b].astype(F32).astype(BF16)
         for later in range(b + 1, batches):
@@ -112,7 +121,7 @@
 
 def assimilate_kernel(
     batches, members, rows_ref, value_ref, error_ref, mask_ref, ens_ref, out_ref,
-    state, result, wide, coef, in_sem, out_sem,
+    state, result, wide, coef, open_mask, sbuf, pbuf, in_sem, out_sem,
 ):
     count = rows_ref.shape[1]
     chunks, halves, _, sub, lanes = state.shape
@@ -157,7 +166,7 @@
             stack = jnp.concatenate([hi, w - hi, hi, spare], axis=0)
             wide[b] = stack.T.astype(BF16)
             hi, low = split(change)
-            coef[b] = jnp.concatenate([hi, hi, low], axis=1)
+            coef[b] = jnp.concatenate([jnp.concatenate([x, x], axis=1) for x in (hi, low)], axis=0)
         return functools.reduce(jnp.minimum, lows)
 
     reached = analyse(solve)
@@ -171,24 +180,40 @@
         for j in range(chunks)
         for h in range(halves)
     ]
+    for b in range(batches):
+        open_mask[b] = mask_ref[b].astype(F32)
+
     for j in range(chunks):
         src, dst = [], []
         for h in range(halves):
             loads[j * halves + h].wait()
             src.append(state.at[j, h].reshape(members * sub, lanes))
             dst.append(result.at[j, h].reshape(members * sub, lanes))
-        for level in range(sub):
-            cells = jnp.concatenate([r[pl.ds(level, members, stride=sub), :] for r in src], axis=1)
+
+        def update(step, _):
+            every = range(LEVELS_AT_ONCE)
+            at = [pl.ds(step * LEVELS_AT_ONCE + k, members, stride=sub) for k in every]
+            cells = [jnp.concatenate([r[at[k], :] for r in src], axis=1) for k in every]
             for b in range(batches):
-                hi, low = split(cells)
-                stack = jnp.concatenate([hi, hi, low], axis=0)
-                proj = mm(wide[b][:, : 3 * members], stack, precision=None)
-                proj = proj * mask_ref[b].astype(F32)
-                hi, low = split(proj)
-                stack = jnp.concatenate([hi, low, hi], axis=0)
-                cells = cells + mm(coef[b], stack, precision=None)
-            for h in range(halves):
-                dst[h][pl.ds(level, members, stride=sub), :] = cells[:, h * lanes : (h + 1) * lanes]
+                for k in every:
+                    hi, low = split(cells[k])
+                    sbuf[k, :members] = hi
+                    sbuf[k, members : 2 * members] = hi
+                    sbuf[k, 2 * members :] = low
+                for k in every:
+                    proj = mm(wide[b][:, : 3 * members], sbuf[k], precision=None)
+                    hi, low = split(proj * open_mask[b])
+                    pbuf[k, :count] = hi
+                    pbuf[k, count:] = low
+                for k in every:
+                    both = mm(coef[b], pbuf[k], precision=None)
+                    cells[k] = cells[k] + (both[:members] + both[members:])
+            for k in every:
+                for h in range(halves):
+                    dst[h][at[k], :] = cells[k][:, h * lanes : (h + 1) * lanes]
+            return 0
+
+        lax.fori_loop(0, sub // LEVELS_AT_ONCE, update, 0)
         for h in range(halves):
             stores[j * halves + h].start()
     for store in stores:
@@ -223,38 +248,40 @@
     used = batches * members + batches * (batches - 1) // 2 * count
     total = -(-used // (8 * n_lon)) * 8 * n_lon
     vmem = pl.BlockSpec(memory_space=pltpu.VMEM)
+    hbm = pl.BlockSpec(memory_space=pltpu.HBM)
     packed = pl.pallas_call(
-        functools.partial(pick_kernel, n_lat, batches),
-        grid=(1,),
+        functools.partial(pick_kernel, n_lat),
         out_shape=jax.ShapeDtypeStruct((total, count), F32),
-        in_specs=[
-            pl.BlockSpec((batches, count), lambda i: (0, 0)),
-            pl.BlockSpec((batches, count), lambda i: (0, 0)),
-            pl.BlockSpec((batches - 1, count, columns), lambda i: (0, 0, 0)),
-        ]
-        + [
-            pl.BlockSpec((members, sub, lanes), functools.partial(lambda h, i: (0, 0, h), h))
-            for h in range(halves)
+        in_specs=[hbm, hbm, hbm, hbm],
+        out_specs=vmem,
+        scratch_shapes=[
+            pltpu.VMEM((batches, count), jnp.int32),
+            pltpu.VMEM((batches, count), jnp.int32),
+            pltpu.VMEM((batches - 1, count, columns), jnp.int32),
+            pltpu.VMEM((members, columns), F32),
+            pltpu.SemaphoreType.DMA((4,)),
         ],
-        out_specs=pl.BlockSpec((total, count), lambda i: (0, 0)),
-        compiler_params=pltpu.CompilerParams(vmem_limit_bytes=VMEM_LIMIT),
+        compiler_params=pltpu.CompilerParams(),
         name="pick",
-    )(obs_block, obs_column, masks, *[field] * halves)
+    )(obs_block, obs_column, masks, field)
     rows = exchange(packed)
     result = pl.pallas_call(
         functools.partial(assimilate_kernel, batches, members),
         out_shape=jax.ShapeDtypeStruct((members, chunks, sub, columns), F32),
-        in_specs=[vmem, vmem, vmem, vmem, pl.BlockSpec(memory_space=pl.ANY)],
-        out_specs=pl.BlockSpec(memory_space=pl.ANY),
+        in_specs=[vmem, vmem, vmem, vmem, hbm],
+        out_specs=hbm,
         scratch_shapes=[
             pltpu.VMEM((chunks, halves, members, sub, lanes), F32),
             pltpu.VMEM((chunks, halves, members, sub, lanes), F32),
             pltpu.VMEM((batches, count, -(-3 * members // 128) * 128), BF16),
-            pltpu.VMEM((batches, members, 3 * count), BF16),
+            pltpu.VMEM((batches, 2 * members, 2 * count), BF16),
+            pltpu.VMEM((batches, count, columns), F32),
+            pltpu.VMEM((LEVELS_AT_ONCE, 3 * members, columns), BF16),
+            pltpu.VMEM((LEVELS_AT_ONCE, 2 * count, columns), BF16),
             pltpu.SemaphoreType.DMA((chunks, halves)),
             pltpu.SemaphoreType.DMA((chunks, halves)),
         ],
-        compiler_params=pltpu.CompilerParams(vmem_limit_bytes=VMEM_LIMIT),
+        compiler_params=pltpu.CompilerParams(),
         name="assimilate",
     )(rows, obs_value, obs_error, masks, field.reshape(members, chunks, sub, columns))
     return result.reshape(ensemble.shape)

time: 62.2 us -> 46.3 us (0.74)
  Pallas kernels: 27.4 us -> 14.8 us
  local copies, waits for them, and re-layouts: 4.11 us -> 0 us
  blocking collectives: 21.2 us -> 22.3 us
    pallas_call x1, Pallas kernels: 27 us -> 12.6 us  [body(): pl.pallas_call(functools.partial(assimilate_kernel, batches, members), ou...]
    unnamed x16 -> x0, local copies, waits for them, and re-layouts: 4.11 us -> none
    pallas_call x1, Pallas kernels: 0.35 us -> 2.17 us  [body(): pl.pallas_call(functools.partial(pick_kernel, n_lat), out_shape=jax.Shape...]
    all_gather x1, blocking collectives: 8.48 us -> 9.49 us  [exchange(): return lax.all_gather(y, 'lon', axis=0, tiled=True)]
where the time goes in v2:
time: 46.3 us; the launch traced here: 46.1 us
  blocking collectives  22.3 us (48%)
  Pallas kernels  14.8 us (32%)
  waiting for transfers between devices  4.73 us (10%)
  starting transfers between devices  4.23 us (9%)
    all_to_all x1, blocking collectives, exchange(): y = lax.all_to_all(parts, 'lon', 0, 0, tiled=True).sum(0)  12.8 us
    pallas_call x1, Pallas kernels, body(): pl.pallas_call(functools.partial(assimilate_kernel, batches, members), ou...  12.6 us
    all_gather x1, blocking collectives, exchange(): return lax.all_gather(y, 'lon', axis=0, tiled=True)  9.49 us
    ppermute x2, waiting for transfers between devices, exchange(): y = y + lax.ppermute(y, 'lat', [(i, i ^ k) for i in range(n_lat)])  4.73 us
    ppermute x2, starting transfers between devices, exchange(): y = y + lax.ppermute(y, 'lat', [(i, i ^ k) for i in range(n_lat)])  4.23 us
    pallas_call x1, Pallas kernels, body(): pl.pallas_call(functools.partial(pick_kernel, n_lat), out_shape=jax.Shape...  2.17 us
  transfers between devices with their start and end apart: 2, of which 2 were waited for; matrix products, arithmetic and copies ran while one was open for 0% of the time, Pallas kernels for 0%

profile of v2, /device:TPU:0, one launch (start us, length us, event | category | flops | bytes accessed | tf_op | source)
XLA Modules:
  0.0 46.1 jit_solution(8489693203896125078)
XLA Ops:
  0.0 2.2 %pick.1 = f32[640,128]{1,0:T(8,128)} custom-call(s32[3,128]{1,0:T(4,128)} %block_hbm.1, s32[3,128]{1,0:T(4,128)} %column_hbm.1, s32[3,128,256]{2,1,0:T(8,128)} %bitcast.7, f32[80,32,256]{2,1,0:T(8,128)} %bitcast.5), custom_call_target="tpu_custom_call" | custom-call | tf_op jit(solution)/shard_map/pick/pallas_call | solution.py:252
  2.2 12.8 %all_to_all.5 = f32[8,80,128]{2,1,0:T(8,128)S(1)} all-to-all(f32[8,80,128]{2,1,0:T(8,128)} %bitcast.9), channel_id=1, replica_groups=mesh['lon'=8,'lat'=4] {'lon'}, dimensions={0} | all-to-all | bytes 655360 | tf_op jit(solution)/shard_map/all_to_all | solution.py:227
  15.0 1.6 %collective-permute-start = (f32[80,128]{1,0:T(8,128)S(1)}, f32[80,128]{1,0:T(8,128)S(1)}, u32[]{:S(2)}, u32[]{:S(2)}) collective-permute-start(f32[80,128]{1,0:T(8,128)S(1)} %reduce_sum.9), channel_id=1, source_target_pairs={{0,1},{1,0},{2,3},{3,2},{4,5},{5,4},{6,7},{7,6},{8,9},{9,8},{10,11... | collective-permute-start | bytes 122888 | tf_op jit(solution)/shard_map/ppermute | solution.py:231
  16.7 2.4 %collective-permute-done = f32[80,128]{1,0:T(8,128)S(1)} collective-permute-done((f32[80,128]{1,0:T(8,128)S(1)}, f32[80,128]{1,0:T(8,128)S(1)}, u32[]{:S(2)}, u32[]{:S(2)}) %collective-permute-start) | collective-permute-done | bytes 40992 | tf_op jit(solution)/shard_map/ppermute | solution.py:231
  19.1 2.6 %collective-permute-start.1 = (f32[80,128]{1,0:T(8,128)S(1)}, f32[80,128]{1,0:T(8,128)S(1)}, u32[]{:S(2)}, u32[]{:S(2)}) collective-permute-start(f32[80,128]{1,0:T(8,128)S(1)} %add.6), channel_id=1, source_target_pairs={{0,2},{1,3},{2,0},{3,1},{4,6},{5,7},{6,4},{7,5},{8,10},{9,11},{10,... | collective-permute-start | bytes 122888 | tf_op jit(solution)/shard_map/ppermute | solution.py:231
  21.7 2.3 %collective-permute-done.1 = f32[80,128]{1,0:T(8,128)S(1)} collective-permute-done((f32[80,128]{1,0:T(8,128)S(1)}, f32[80,128]{1,0:T(8,128)S(1)}, u32[]{:S(2)}, u32[]{:S(2)}) %collective-permute-start.1) | collective-permute-done | bytes 40992 | tf_op jit(solution)/shard_map/ppermute | solution.py:231
  24.0 9.5 %all_gather.3.rows_ref = f32[640,128]{1,0:T(8,128)} all-gather(f32[80,128]{1,0:T(8,128)S(1)} %add.7), channel_id=1, replica_groups=mesh['lon'=8,'lat'=4] {'lon'}, dimensions={0}, use_global_device_ids=true | all-gather | bytes 368640 | tf_op jit(solution)/shard_map/all_gather | solution.py:235
  33.5 12.6 %assimilate.1 = f32[80,4,8,256]{3,2,1,0:T(8,128)} custom-call(f32[640,128]{1,0:T(8,128)} %all_gather.3.rows_ref, f32[3,128]{1,0:T(4,128)} %value_ref.1, f32[3,128]{1,0:T(4,128)} %error_ref.1, s32[3,128,256]{2,1,0:T(8,128)} %bitcast.8, f32[80,4,8,256]{3,2,1,0:T(8,128)} %bitcast.6), custom_call_target="tpu_custom_call" | custom-call | tf_op jit(solution)/shard_map/assimilate/pallas_call | solution.py:268
  (3 shorter events, 0.0 us)
Async XLA Ops:
  15.0 4.1 %collective-permute-start = (f32[80,128]{1,0:T(8,128)S(1)}, f32[80,128]{1,0:T(8,128)S(1)}, u32[]{:S(2)}, u32[]{:S(2)}) collective-permute-start(f32[80,128]{1,0:T(8,128)S(1)} %reduce_sum.9), channel_id=1, source_target_pairs={{0,1},{1,0},{2,3},{3,2},{4,5},{5,4},{6,7},{7,6},{8,9},{9,8},{10,11... | collective-permute-start | bytes 122888 | tf_op jit(solution)/shard_map/ppermute | solution.py:231
  19.1 4.9 %collective-permute-start.1 = (f32[80,128]{1,0:T(8,128)S(1)}, f32[80,128]{1,0:T(8,128)S(1)}, u32[]{:S(2)}, u32[]{:S(2)}) collective-permute-start(f32[80,128]{1,0:T(8,128)S(1)} %add.6), channel_id=1, source_target_pairs={{0,2},{1,3},{2,0},{3,1},{4,6},{5,7},{6,4},{7,5},{8,10},{9,11},{10,... | collective-permute-start | bytes 122888 | tf_op jit(solution)/shard_map/ppermute | solution.py:231

commit v3 on v2

v3 whole, which is shorter than its diff:
```python
import functools
import jax
import jax.numpy as jnp
from jax import lax
from jax.experimental import pallas as pl
from jax.experimental.pallas import tpu as pltpu
from jax.sharding import PartitionSpec as P

F32 = jnp.float32
BF16 = jnp.bfloat16
HIGHEST = lax.Precision.HIGHEST
DOUBLINGS = 6
LEVELS_AT_ONCE = 8
ENOUGH = 2.0**25
VMEM_LIMIT = 56_000_000


def mm(a, b, contract=((1,), (0,)), precision=HIGHEST):
    return lax.dot_general(
        a, b, (contract, ((), ())), precision=precision, preferred_element_type=F32
    )


def mm3(a, b, contract=((1,), (0,))):
    product = functools.partial(mm, contract=contract, precision=None)
    return product(a[0], b[0]) + (product(a[0], b[1]) + product(a[1], b[0]))


def split(x):
    hi = x.astype(BF16)
    return hi, (x - hi.astype(F32)).astype(BF16)


def pick_kernel(
    n_lat, direct, block_hbm, column_hbm, mask_hbm, ens_hbm, *refs
):
    out_refs, (out_ref, block_ref, column_ref, mask_ref, surface_ref, sems) = refs[:-6], refs[-6:]
    batches, count = block_ref.shape
    members, columns = surface_ref.shape
    pairs = [
        (block_hbm, block_ref),
        (column_hbm, column_ref),
        (ens_hbm.at[:, 0, :], surface_ref),
        (mask_hbm.at[: batches - 1], mask_ref),
    ]
    copies = [pltpu.make_async_copy(a, b, sems.at[i]) for i, (a, b) in enumerate(pairs)]
    for copy in copies:
        copy.start()
    here = lax.axis_index("lon") * n_lat + lax.axis_index("lat")
    ids = lax.broadcasted_iota(jnp.int32, (columns, count), 0)
    copies[0].wait()
    copies[1].wait()
    picks = []
    for b in range(batches):
        key = jnp.where(block_ref[b : b + 1] == here, column_ref[b : b + 1], -1)
        picks.append((ids == key).astype(F32).astype(BF16))
    copies[2].wait()
    surface = surface_ref[...]
    hi = surface.astype(BF16)
    rest = surface - hi.astype(F32)
    mid = rest.astype(BF16)
    low = (rest - mid.astype(F32)).astype(BF16)
    lon = lax.axis_index("lon")

    def put(at, value):
        if not direct:
            out_ref[at : at + value.shape[0], :] = value
            return
        done, size = 0, out_ref.shape[2]
        while done < value.shape[0]:
            block, start = divmod(at + done, size)
            take = min(size - start, value.shape[0] - done)
            core, plane = (block % 2) ^ (lon % 2), (block // 2) ^ (lon // 2)
            out_ref[core, plane, start : start + take, :] = value[done : done + take]
            done += take

    at = 0
    for b in range(batches):
        parts = [mm(part, picks[b], precision=None) for part in (hi, mid, low)]
        put(at, (parts[2] + parts[1]) + parts[0])
        at += members
    copies[3].wait()
    for b in range(batches - 1):
        entries = mask_ref[b].astype(F32).astype(BF16)
        for later in range(b + 1, batches):
            put(at, mm(entries, picks[later], precision=None))
            at += count
    rows = out_ref.size // count
    if at < rows:
        put(at, jnp.zeros((rows - at, count), F32))
    if direct:
        out_refs[0][...] = out_ref[1]
        for k, ref in enumerate(out_refs[1:]):
            ref[...] = out_ref[0, k]
    else:
        out_refs[0][...] = out_ref[...]


def bounds(gram):
    norm = jnp.sum(jnp.sum(gram * gram, axis=0, keepdims=True), axis=1, keepdims=True)
    return 1.0 + jnp.maximum(jnp.sqrt(norm) * 1.0001, 0.25)


def solve(w, onto, eye):
    ws = split(w)
    gram = mm(w, w, ((1,), (1,)))
    gs = split(gram)
    gram2 = mm3(gs, gs)
    gw = mm3(gs, ws)
    top = bounds(gram)
    alpha = 2.0 / (top + 1.0)
    beta = 1.0 - alpha
    t = (top + 1.0) / (top - 1.0)
    t = 2.0 * t * t - 1.0
    d = 1.0 / t
    v = (1.0 + d) * alpha * (w + (beta * w - alpha * gw))
    e = (1.0 + d) * (
        (beta * beta) * eye - (2.0 * alpha * beta) * gram + (alpha * alpha) * gram2
    ) - d * eye
    for step in range(1, DOUBLINGS):
        t = jnp.minimum(2.0 * t * t - 1.0, 1e15)
        d = 1.0 / t
        es = split(e)
        last = step == DOUBLINGS - 1
        if last and onto is not None:
            onto = mm3(split(v), split(onto))
            onto = (1.0 + d) * (onto + mm3(es, split(onto)))
        v = (1.0 + d) * (v + mm3(es, split(v)))
        if not last:
            e = (1.0 + d) * mm3(es, es) - d * eye
    return v, onto, t


def solve_long(w, onto, eye):
    gram = mm(w, w, ((1,), (1,)))
    top = bounds(gram)
    alpha = 2.0 / (top + 1.0)

    def more(carry):
        return carry[2][0, 0] < ENOUGH

    def double(carry):
        e, x, t = carry
        t = jnp.minimum(2.0 * t * t - 1.0, 1e15)
        d = 1.0 / t
        return (1.0 + d) * mm(e, e) - d * eye, (1.0 + d) * (x + mm(e, x)), t

    e = (1.0 - alpha) * eye - alpha * gram
    x = alpha * eye
    x = lax.while_loop(more, double, (e, x, (top + 1.0) / (top - 1.0)))[1]

    def correct(_, v):
        return v + mm(x, w - (v + mm(gram, v)))

    v = lax.fori_loop(0, 3, correct, mm(x, w))
    return v, None if onto is None else mm(v, onto), jnp.ones((1, 1), F32)


def assimilate_kernel(
    batches, members, rows_ref, value_ref, error_ref, mask_hbm, ens_ref, out_ref,
    state, result, wide, coef, open_mask, sbuf, pbuf, mask_ref, in_sem, out_sem, mask_sem,
):
    count = rows_ref.shape[1]
    chunks, halves, _, sub, lanes = state.shape

    def piece(ref, j, h):
        return ref.at[:, j, :, h * lanes : (h + 1) * lanes]

    loads = [
        pltpu.make_async_copy(piece(ens_ref, j, h), state.at[j, h], in_sem.at[j, h])
        for j in range(chunks)
        for h in range(halves)
    ]
    for load in loads:
        load.start()
    mask_load = pltpu.make_async_copy(mask_hbm, mask_ref, mask_sem)
    mask_load.start()
    scale = 1.0 / jnp.sqrt(jnp.full((1, 1), members - 1, F32))
    eye = (
        lax.broadcasted_iota(jnp.int32, (members, members), 0)
        == lax.broadcasted_iota(jnp.int32, (members, members), 1)
    ).astype(F32)
    def analyse(solver, b, obs):
        mean = jnp.mean(obs[b], axis=0, keepdims=True)
        errors = error_ref[b : b + 1]
        w = (obs[b] - mean) * scale / errors
        raw = (value_ref[b : b + 1] - mean) / errors
        along = jnp.sum(w * raw, axis=1, keepdims=True)
        at = batches * members + sum(batches - 1 - k for k in range(b)) * count
        ws = split(w)
        onto = []
        for later in range(b + 1, batches):
            onto.append(rows_ref[at : at + count, :] * mm3(ws, split(obs[later]), ((0,), (0,))))
            at += count
        onto = jnp.concatenate(onto, axis=1) if onto else None
        v, moved, t = solver(w, onto, eye)
        if onto is not None:
            mean_move = jnp.sum(raw.T * onto, axis=0, keepdims=True) - jnp.sum(
                along * moved, axis=0, keepdims=True
            )
            moved = scale * mean_move - 0.5 * moved
            for k, later in enumerate(range(b + 1, batches)):
                obs[later] = obs[later] + moved[:, k * count : (k + 1) * count]
        innov = raw - jnp.sum(v * along, axis=0, keepdims=True)
        change = scale * innov - 0.5 * v
        hi = ws[0].astype(F32)
        spare = jnp.zeros((wide.shape[2] - 3 * members, count), F32)
        wide[b] = jnp.concatenate([hi, w - hi, hi, spare], axis=0).T.astype(BF16)
        coef[b] = jnp.concatenate([jnp.concatenate([x, x], axis=1) for x in split(change)], axis=0)
        return t

    def lines(ref, j):
        return [ref.at[j, h].reshape(members * sub, lanes) for h in range(halves)]

    def update(levels):
        every = list(range(len(levels)))
        src = [lines(state, j) for j, _ in levels]
        dst = [lines(result, j) for j, _ in levels]
        at = [pl.ds(level, members, stride=sub) for _, level in levels]
        cells = [jnp.concatenate([r[at[k], :] for r in src[k]], axis=1) for k in every]

        def first(b, k):
            hi, low = split(cells[k])
            sbuf[k, :members] = hi
            sbuf[k, members:] = low
            stack = jnp.concatenate([sbuf[k, :members], sbuf[k]], axis=0)
            proj = mm(wide[b][:, : 3 * members], stack, precision=None)
            hi, low = split(proj * open_mask[b])
            pbuf[k, :count] = hi
            pbuf[k, count:] = low

        def second(b, k):
            both = mm(coef[b], pbuf[k], precision=None)
            cells[k] = cells[k] + (both[:members] + both[members:])

        for b in range(batches):
            for k in every:
                first(b, k)
            for k in every:
                second(b, k)
        for k in every:
            for h in range(halves):
                dst[k][h][at[k], :] = cells[k][:, h * lanes : (h + 1) * lanes]

    def begin():
        return [rows_ref[b * members : (b + 1) * members, :] for b in range(batches)]

    obs = begin()
    reached = functools.reduce(jnp.minimum, [analyse(solve, b, obs) for b in range(batches)])

    @pl.when(jnp.logical_not(reached[0, 0] >= ENOUGH))
    def _():
        obs = begin()
        for b in range(batches):
            analyse(solve_long, b, obs)

    mask_load.wait()
    for b in range(batches):
        open_mask[b] = mask_ref[b].astype(F32)

    stores = [
        pltpu.make_async_copy(result.at[j, h], piece(out_ref, j, h), out_sem.at[j, h])
        for j in range(chunks)
        for h in range(halves)
    ]
    group = LEVELS_AT_ONCE // sub
    for j0 in range(0, chunks, group):
        js = range(j0, min(j0 + group, chunks))
        for j in js:
            for h in range(halves):
                loads[j * halves + h].wait()
        update([(j, level) for j in js for level in range(sub)])
        for j in js:
            for h in range(halves):
                stores[j * halves + h].start()
    for store in stores:
        store.wait()


def exchange(x):
    n_lon = lax.axis_size("lon")
    n_lat = lax.axis_size("lat")
    if len(x) > 1:
        met = lax.ppermute(x[0], "lon", [(i, i ^ 1) for i in range(n_lon)])
        y = [own + met[k] for k, own in enumerate(x[1:])]
        terms = [
            lax.ppermute(y[k], "lon", [(i, i ^ (2 * k)) for i in range(n_lon)])
            for k in range(1, n_lon // 2)
        ]
        y = functools.reduce(jnp.add, terms, y[0])
    else:
        parts = x[0].reshape(n_lon, x[0].shape[0] // n_lon, x[0].shape[1])
        y = lax.all_to_all(parts, "lon", 0, 0, tiled=True).sum(0)
    if n_lat <= 4:
        ring = [[(i, (i + k) % n_lat) for i in range(n_lat)] for k in range(1, n_lat)]
        if n_lat & (n_lat - 1) == 0:
            ring = [[(i, i ^ k) for i in range(n_lat)] for k in range(1, n_lat)]
        y = functools.reduce(jnp.add, [lax.ppermute(y, "lat", pairs) for pairs in ring], y)
    elif n_lat & (n_lat - 1) == 0:
        k = 1
        while k < n_lat:
            y = y + lax.ppermute(y, "lat", [(i, i ^ k) for i in range(n_lat)])
            k *= 2
    else:
        y = lax.psum(y, "lat")
    return lax.all_gather(y, "lon", axis=0, tiled=True)


def body(ensemble, obs_block, obs_column, obs_value, obs_error, loc_mask):
    members, levels, columns = ensemble.shape[2:]
    batches, count = obs_block.shape
    n_lon = lax.axis_size("lon")
    n_lat = lax.axis_size("lat")
    sub, lanes = 8, 128
    halves = columns // lanes
    chunks = levels // sub
    field = ensemble.reshape(members, levels, columns)
    masks = loc_mask.reshape(batches, count, columns)
    used = batches * members + batches * (batches - 1) // 2 * count
    total = -(-used // (8 * n_lon)) * 8 * n_lon
    direct = n_lon in (2, 4, 8)
    packed_shape = (2, n_lon // 2, total // n_lon, count) if direct else (total, count)
    shapes = [packed_shape[1:]] + [packed_shape[2:]] * packed_shape[1] if direct else [packed_shape]
    vmem = pl.BlockSpec(memory_space=pltpu.VMEM)
    hbm = pl.BlockSpec(memory_space=pltpu.HBM)
    packed = pl.pallas_call(
        functools.partial(pick_kernel, n_lat, direct),
        out_shape=[jax.ShapeDtypeStruct(shape, F32) for shape in shapes],
        in_specs=[hbm, hbm, hbm, hbm],
        out_specs=[vmem] * len(shapes),
        scratch_shapes=[
            pltpu.VMEM(packed_shape, F32),
            pltpu.VMEM((batches, count), jnp.int32),
            pltpu.VMEM((batches, count), jnp.int32),
            pltpu.VMEM((batches - 1, count, columns), jnp.int32),
            pltpu.VMEM((members, columns), F32),
            pltpu.SemaphoreType.DMA((4,)),
        ],
        compiler_params=pltpu.CompilerParams(vmem_limit_bytes=VMEM_LIMIT),
        name="pick",
    )(obs_block, obs_column, masks, field)
    rows = exchange(packed)
    result = pl.pallas_call(
        functools.partial(assimilate_kernel, batches, members),
        out_shape=jax.ShapeDtypeStruct((members, chunks, sub, columns), F32),
        in_specs=[vmem, vmem, vmem, hbm, hbm],
        out_specs=hbm,
        scratch_shapes=[
            pltpu.VMEM((chunks, halves, members, sub, lanes), F32),
            pltpu.VMEM((chunks, halves, members, sub, lanes), F32),
            pltpu.VMEM((batches, count, -(-3 * members // 128) * 128), BF16),
            pltpu.VMEM((batches, 2 * members, 2 * count), BF16),
            pltpu.VMEM((batches, count, columns), F32),
            pltpu.VMEM((LEVELS_AT_ONCE, 2 * members, columns), BF16),
            pltpu.VMEM((LEVELS_AT_ONCE, 2 * count, columns), BF16),
            pltpu.VMEM((batches, count, columns), jnp.int32),
            pltpu.SemaphoreType.DMA((chunks, halves)),
            pltpu.SemaphoreType.DMA((chunks, halves)),
            pltpu.SemaphoreType.DMA,
        ],
        compiler_params=pltpu.CompilerParams(vmem_limit_bytes=VMEM_LIMIT),
        name="assimilate",
    )(rows, obs_value, obs_error, masks, field.reshape(members, chunks, sub, columns))
    return result.reshape(ensemble.shape)


def solution(mesh):
    placed = (
        P("lon", "lat", None, None, None),
        P(),
        P(),
        P(),
        P(),
        P("lon", "lat", None, None, None),
    )
    return jax.shard_map(
        body,
        mesh=mesh,
        in_specs=placed,
        out_specs=P("lon", "lat", None, None, None),
        check_vma=False,
    )
```

time: 46.3 us -> 42.4 us (0.916)
  blocking collectives: 22.3 us -> 9.42 us
  starting transfers between devices: 4.23 us -> 9.45 us
  waiting for transfers between devices: 4.73 us -> 9.1 us
  Pallas kernels: 14.8 us -> 12.8 us
  local copies, waits for them, and re-layouts: 0 us -> 1.4 us
    all_to_all x1 -> x0, blocking collectives: 12.8 us -> none  [exchange(): y = lax.all_to_all(parts, 'lon', 0, 0, tiled=True).sum(0)]
    ppermute x2 -> x7, starting transfers between devices: 4.23 us -> 9.45 us  [the longest x3 4.45 us: exchange(): lax.ppermute(y, 'lat', pairs)]
    ppermute x2 -> x7, waiting for transfers between devices: 4.73 us -> 9.1 us  [the longest x3 4.12 us: exchange(): lax.ppermute(y, 'lat', pairs)]
    unnamed x0 -> x8, local copies, waits for them, and re-layouts: none -> 1.4 us
    pallas_call x1, Pallas kernels: 12.6 us -> 11.3 us  [body(): pl.pallas_call(functools.partial(assimilate_kernel, batches, members), ou...]
    pallas_call x1, Pallas kernels: 2.17 us -> 1.45 us  [body(): pl.pallas_call(functools.partial(pick_kernel, n_lat, direct), out_shape=[...]
  transfers between devices with their start and end apart: 2 -> 7, of which waited for: 2 -> 6; matrix products, arithmetic and copies ran while one was open for 0% -> 0% of each run, Pallas kernels for 0% -> 0%
where the time goes in v3:
time: 42.4 us; the launch traced here: 42.2 us
  Pallas kernels  12.8 us (30%)
  starting transfers between devices  9.45 us (22%)
  blocking collectives  9.42 us (22%)
  waiting for transfers between devices  9.1 us (21%)
  local copies, waits for them, and re-layouts  1.4 us (3%)
    pallas_call x1, Pallas kernels, body(): pl.pallas_call(functools.partial(assimilate_kernel, batches, members), ou...  11.3 us
    all_gather x1, blocking collectives, exchange(): return lax.all_gather(y, 'lon', axis=0, tiled=True)  9.42 us
    ppermute x3, starting transfers between devices, exchange(): lax.ppermute(y, 'lat', pairs)  4.45 us
    ppermute x3, starting transfers between devices, exchange(): lax.ppermute(y[k], 'lon', [(i, i ^ 2 * k) for i in range(n_lon)])  4.44 us
    ppermute x3, waiting for transfers between devices, exchange(): lax.ppermute(y, 'lat', pairs)  4.12 us
    ppermute x3, waiting for transfers between devices, exchange(): lax.ppermute(y[k], 'lon', [(i, i ^ 2 * k) for i in range(n_lon)])  3.95 us
    pallas_call x1, Pallas kernels, body(): pl.pallas_call(functools.partial(pick_kernel, n_lat, direct), out_shape=[...  1.45 us
    unnamed x8, local copies, waits for them, and re-layouts  1.4 us
  transfers between devices with their start and end apart: 7, of which 6 were waited for; matrix products, arithmetic and copies ran while one was open for 0% of the time, Pallas kernels for 0%

profile of v3, /device:TPU:0, one launch (start us, length us, event | category | flops | bytes accessed | tf_op | source)
XLA Modules:
  0.0 42.2 jit_solution(843915328681525392)
XLA Ops:
  0.0 0.0 copy-start.1
  0.0 0.0 copy-start
  0.0 0.0 copy-start.2
  0.0 0.7 %copy-done.2 = s32[3,128]{1,0:T(4,128)S(1)} copy-done((s32[3,128]{1,0:T(4,128)S(1)}, s32[3,128]{1,0:T(4,128)}, u32[]{:S(2)}) %copy-start.2) | copy-done | bytes 1560
  0.7 0.0 copy-start.3
  0.7 0.7 %copy-done.3 = s32[3,128]{1,0:T(4,128)S(1)} copy-done((s32[3,128]{1,0:T(4,128)S(1)}, s32[3,128]{1,0:T(4,128)}, u32[]{:S(2)}) %copy-start.3) | copy-done | bytes 1560
  1.4 1.4 %pick.1 = (f32[4,80,128]{2,1,0:T(8,128)S(1)}, f32[80,128]{1,0:T(8,128)S(1)}, f32[80,128]{1,0:T(8,128)S(1)}, f32[80,128]{1,0:T(8,128)S(1)}, f32[80,128]{1,0:T(8,128)S(1)}) custom-call(s32[3,128]{1,0:T(4,128)S(1)} %copy-done.2, s32[3,128]{1,0:T(4,128)S(1)} %copy-done.3, s32[3,128,256]{2,1,0:T(8,128)} %bitcast.28, f32[80,32,256]{2,1,0:T(8,128)} %bitcast.26), custom_call_target="tpu_custom_call" | custom-call | tf_op jit(solution)/shard_map/pick/pallas_call | solution.py:326
  2.9 0.6 %collective-permute-start = (f32[4,80,128]{2,1,0:T(8,128)S(1)}, f32[4,80,128]{2,1,0:T(8,128)S(1)}, u32[]{:S(2)}, u32[]{:S(2)}) collective-permute-start(f32[4,80,128]{2,1,0:T(8,128)S(1)} %get-tuple-element.11), channel_id=1, source_target_pairs={{0,4},{4,0},{8,12},{12,8},{16,20},{20,16},{24,28},{28,24},{1,5},{5... | collective-permute-start | bytes 491528 | tf_op jit(solution)/shard_map/ppermute | solution.py:284
  3.4 1.0 %collective-permute-done = f32[4,80,128]{2,1,0:T(8,128)S(1)} collective-permute-done((f32[4,80,128]{2,1,0:T(8,128)S(1)}, f32[4,80,128]{2,1,0:T(8,128)S(1)}, u32[]{:S(2)}, u32[]{:S(2)}) %collective-permute-start) | collective-permute-done | bytes 163872 | tf_op jit(solution)/shard_map/ppermute | solution.py:284
  4.5 2.9 %collective-permute-start.1 = (f32[80,128]{1,0:T(8,128)S(1)}, f32[80,128]{1,0:T(8,128)S(1)}, u32[]{:S(2)}, u32[]{:S(2)}) collective-permute-start(f32[80,128]{1,0:T(8,128)S(1)} %get-tuple-element.15), channel_id=1, source_target_pairs={{0,8},{4,12},{8,0},{12,4},{16,24},{20,28},{24,16},{28,20},{1,9},{5... | collective-permute-start | bytes 122888 | tf_op jit(solution)/shard_map/ppermute | solution.py:287
  7.4 1.5 %collective-permute-start.3 = (f32[80,128]{1,0:T(8,128)S(1)}, f32[80,128]{1,0:T(8,128)S(1)}, u32[]{:S(2)}, u32[]{:S(2)}) collective-permute-start(f32[80,128]{1,0:T(8,128)S(1)} %get-tuple-element.16), channel_id=1, source_target_pairs={{0,24},{4,28},{8,16},{12,20},{16,8},{20,12},{24,0},{28,4},{1,25},{... | collective-permute-start | bytes 122888 | tf_op jit(solution)/shard_map/ppermute | solution.py:287
  8.9 0.0 collective-permute-start.2
  8.9 0.4 %collective-permute-done.1 = f32[80,128]{1,0:T(8,128)S(1)} collective-permute-done((f32[80,128]{1,0:T(8,128)S(1)}, f32[80,128]{1,0:T(8,128)S(1)}, u32[]{:S(2)}, u32[]{:S(2)}) %collective-permute-start.1) | collective-permute-done | bytes 40992 | tf_op jit(solution)/shard_map/ppermute | solution.py:287
  9.3 2.9 %collective-permute-done.3 = f32[80,128]{1,0:T(8,128)S(1)} collective-permute-done((f32[80,128]{1,0:T(8,128)S(1)}, f32[80,128]{1,0:T(8,128)S(1)}, u32[]{:S(2)}, u32[]{:S(2)}) %collective-permute-start.3) | collective-permute-done | bytes 40992 | tf_op jit(solution)/shard_map/ppermute | solution.py:287
  12.3 0.6 %collective-permute-done.2 = f32[80,128]{1,0:T(8,128)S(1)} collective-permute-done((f32[80,128]{1,0:T(8,128)S(1)}, f32[80,128]{1,0:T(8,128)S(1)}, u32[]{:S(2)}, u32[]{:S(2)}) %collective-permute-start.2) | collective-permute-done | bytes 40992 | tf_op jit(solution)/shard_map/ppermute | solution.py:287
  12.9 3.7 %collective-permute-start.6 = (f32[80,128]{1,0:T(8,128)S(1)}, f32[80,128]{1,0:T(8,128)S(1)}, u32[]{:S(2)}, u32[]{:S(2)}) collective-permute-start(f32[80,128]{1,0:T(8,128)S(1)} %fusion.6), channel_id=1, source_target_pairs={{0,3},{1,2},{2,1},{3,0},{4,7},{5,6},{6,5},{7,4},{8,11},{9,10},{10,... | collective-permute-start | bytes 122888 | tf_op jit(solution)/shard_map/ppermute | solution.py:298
  16.5 0.0 collective-permute-start.5
  16.5 0.8 %collective-permute-start.4 = (f32[80,128]{1,0:T(8,128)S(1)}, f32[80,128]{1,0:T(8,128)S(1)}, u32[]{:S(2)}, u32[]{:S(2)}) collective-permute-start(f32[80,128]{1,0:T(8,128)S(1)} %fusion.6), channel_id=1, source_target_pairs={{0,1},{1,0},{2,3},{3,2},{4,5},{5,4},{6,7},{7,6},{8,9},{9,8},{10,11... | collective-permute-start | bytes 122888 | tf_op jit(solution)/shard_map/ppermute | solution.py:298
  17.3 1.4 %collective-permute-done.6 = f32[80,128]{1,0:T(8,128)S(1)} collective-permute-done((f32[80,128]{1,0:T(8,128)S(1)}, f32[80,128]{1,0:T(8,128)S(1)}, u32[]{:S(2)}, u32[]{:S(2)}) %collective-permute-start.6) | collective-permute-done | bytes 40992 | tf_op jit(solution)/shard_map/ppermute | solution.py:298
  18.7 2.7 %collective-permute-done.5 = f32[80,128]{1,0:T(8,128)S(1)} collective-permute-done((f32[80,128]{1,0:T(8,128)S(1)}, f32[80,128]{1,0:T(8,128)S(1)}, u32[]{:S(2)}, u32[]{:S(2)}) %collective-permute-start.5) | collective-permute-done | bytes 40992 | tf_op jit(solution)/shard_map/ppermute | solution.py:298
  21.4 0.0 collective-permute-done.4
  21.5 9.4 %all_gather.3.rows_ref = f32[640,128]{1,0:T(8,128)S(1)} all-gather(f32[80,128]{1,0:T(8,128)S(1)} %add_add_fusion), channel_id=1, replica_groups=mesh['lon'=8,'lat'=4] {'lon'}, dimensions={0}, use_global_device_ids=true | all-gather | bytes 368640 | tf_op jit(solution)/shard_map/all_gather | solution.py:306
  30.9 0.0 copy-done.1
  30.9 0.0 copy-done
  30.9 11.3 %assimilate.1 = f32[80,4,8,256]{3,2,1,0:T(8,128)} custom-call(f32[640,128]{1,0:T(8,128)S(1)} %all_gather.3.rows_ref, f32[3,128]{1,0:T(4,128)S(1)} %copy-done, f32[3,128]{1,0:T(4,128)S(1)} %copy-done.1, s32[3,128,256]{2,1,0:T(8,128)} %bitcast.29, f32[80,4,8,256]{3,2,1,0:T(8,128)} %bitcast.27), custom_call_target="tpu_custom_call" | custom-call | tf_op jit(solution)/shard_map/assimilate/pallas_call | solution.py:343
  (3 shorter events, 0.1 us)
Async XLA Ops:
  0.0 30.9 %copy-start.1 = (f32[3,128]{1,0:T(4,128)S(1)}, f32[3,128]{1,0:T(4,128)}, u32[]{:S(2)}) copy-start(f32[3,128]{1,0:T(4,128)} %error_ref.1) | copy-start | bytes 4612
  0.0 30.9 %copy-start = (f32[3,128]{1,0:T(4,128)S(1)}, f32[3,128]{1,0:T(4,128)}, u32[]{:S(2)}) copy-start(f32[3,128]{1,0:T(4,128)} %value_ref.1) | copy-start | bytes 4612
  0.0 0.7 %copy-start.2 = (s32[3,128]{1,0:T(4,128)S(1)}, s32[3,128]{1,0:T(4,128)}, u32[]{:S(2)}) copy-start(s32[3,128]{1,0:T(4,128)} %block_hbm.1) | copy-start | bytes 4612
  0.7 0.7 %copy-start.3 = (s32[3,128]{1,0:T(4,128)S(1)}, s32[3,128]{1,0:T(4,128)}, u32[]{:S(2)}) copy-start(s32[3,128]{1,0:T(4,128)} %column_hbm.1) | copy-start | bytes 4612
  2.9 1.6 %collective-permute-start = (f32[4,80,128]{2,1,0:T(8,128)S(1)}, f32[4,80,128]{2,1,0:T(8,128)S(1)}, u32[]{:S(2)}, u32[]{:S(2)}) collective-permute-start(f32[4,80,128]{2,1,0:T(8,128)S(1)} %get-tuple-element.11), channel_id=1, source_target_pairs={{0,4},{4,0},{8,12},{12,8},{16,20},{20,16},{24,28},{28,24},{1,5},{5... | collective-permute-start | bytes 491528 | tf_op jit(solution)/shard_map/ppermute | solution.py:284
  4.5 4.9 %collective-permute-start.1 = (f32[80,128]{1,0:T(8,128)S(1)}, f32[80,128]{1,0:T(8,128)S(1)}, u32[]{:S(2)}, u32[]{:S(2)}) collective-permute-start(f32[80,128]{1,0:T(8,128)S(1)} %get-tuple-element.15), channel_id=1, source_target_pairs={{0,8},{4,12},{8,0},{12,4},{16,24},{20,28},{24,16},{28,20},{1,9},{5... | collective-permute-start | bytes 122888 | tf_op jit(solution)/shard_map/ppermute | solution.py:287
  7.4 4.9 %collective-permute-start.3 = (f32[80,128]{1,0:T(8,128)S(1)}, f32[80,128]{1,0:T(8,128)S(1)}, u32[]{:S(2)}, u32[]{:S(2)}) collective-permute-start(f32[80,128]{1,0:T(8,128)S(1)} %get-tuple-element.16), channel_id=1, source_target_pairs={{0,24},{4,28},{8,16},{12,20},{16,8},{20,12},{24,0},{28,4},{1,25},{... | collective-permute-start | bytes 122888 | tf_op jit(solution)/shard_map/ppermute | solution.py:287
  8.9 4.0 %collective-permute-start.2 = (f32[80,128]{1,0:T(8,128)S(1)}, f32[80,128]{1,0:T(8,128)S(1)}, u32[]{:S(2)}, u32[]{:S(2)}) collective-permute-start(f32[80,128]{1,0:T(8,128)S(1)} %get-tuple-element.17), channel_id=1, source_target_pairs={{0,16},{4,20},{8,24},{12,28},{16,0},{20,4},{24,8},{28,12},{1,17},{... | collective-permute-start | bytes 122888 | tf_op jit(solution)/shard_map/ppermute | solution.py:287
  12.9 5.9 %collective-permute-start.6 = (f32[80,128]{1,0:T(8,128)S(1)}, f32[80,128]{1,0:T(8,128)S(1)}, u32[]{:S(2)}, u32[]{:S(2)}) collective-permute-start(f32[80,128]{1,0:T(8,128)S(1)} %fusion.6), channel_id=1, source_target_pairs={{0,3},{1,2},{2,1},{3,0},{4,7},{5,6},{6,5},{7,4},{8,11},{9,10},{10,... | collective-permute-start | bytes 122888 | tf_op jit(solution)/shard_map/ppermute | solution.py:298
  16.5 4.9 %collective-permute-start.5 = (f32[80,128]{1,0:T(8,128)S(1)}, f32[80,128]{1,0:T(8,128)S(1)}, u32[]{:S(2)}, u32[]{:S(2)}) collective-permute-start(f32[80,128]{1,0:T(8,128)S(1)} %fusion.6), channel_id=1, source_target_pairs={{0,2},{1,3},{2,0},{3,1},{4,6},{5,7},{6,4},{7,5},{8,10},{9,11},{10,... | collective-permute-start | bytes 122888 | tf_op jit(solution)/shard_map/ppermute | solution.py:298
  16.5 4.9 %collective-permute-start.4 = (f32[80,128]{1,0:T(8,128)S(1)}, f32[80,128]{1,0:T(8,128)S(1)}, u32[]{:S(2)}, u32[]{:S(2)}) collective-permute-start(f32[80,128]{1,0:T(8,128)S(1)} %fusion.6), channel_id=1, source_target_pairs={{0,1},{1,0},{2,3},{3,2},{4,5},{5,4},{6,7},{7,6},{8,9},{9,8},{10,11... | collective-permute-start | bytes 122888 | tf_op jit(solution)/shard_map/ppermute | solution.py:298

commit v4 on v3

--- a/solution.py
+++ b/solution.py
@@ -11,6 +11,7 @@
 HIGHEST = lax.Precision.HIGHEST
 DOUBLINGS = 6
 LEVELS_AT_ONCE = 8
+ABREAST = 2
 ENOUGH = 2.0**25
 VMEM_LIMIT = 56_000_000
 
@@ -32,29 +33,25 @@
 
 
 def pick_kernel(
-    n_lat, direct, block_hbm, column_hbm, mask_hbm, ens_hbm, *refs
+    direct, key_hbm, mask_hbm, ens_hbm, *refs
 ):
-    out_refs, (out_ref, block_ref, column_ref, mask_ref, surface_ref, sems) = refs[:-6], refs[-6:]
-    batches, count = block_ref.shape
+    out_refs, (out_ref, key_ref, mask_ref, surface_ref, sems) = refs[:-5], refs[-5:]
+    batches, count = key_ref.shape
     members, columns = surface_ref.shape
     pairs = [
-        (block_hbm, block_ref),
-        (column_hbm, column_ref),
+        (key_hbm, key_ref),
         (ens_hbm.at[:, 0, :], surface_ref),
         (mask_hbm.at[: batches - 1], mask_ref),
     ]
     copies = [pltpu.make_async_copy(a, b, sems.at[i]) for i, (a, b) in enumerate(pairs)]
     for copy in copies:
         copy.start()
-    here = lax.axis_index("lon") * n_lat + lax.axis_index("lat")
     ids = lax.broadcasted_iota(jnp.int32, (columns, count), 0)
     copies[0].wait()
-    copies[1].wait()
     picks = []
     for b in range(batches):
-        key = jnp.where(block_ref[b : b + 1] == here, column_ref[b : b + 1], -1)
-        picks.append((ids == key).astype(F32).astype(BF16))
-    copies[2].wait()
+        picks.append((ids == key_ref[b : b + 1]).astype(F32).astype(BF16))
+    copies[1].wait()
     surface = surface_ref[...]
     hi = surface.astype(BF16)
     rest = surface - hi.astype(F32)
@@ -79,7 +76,7 @@
         parts = [mm(part, picks[b], precision=None) for part in (hi, mid, low)]
         put(at, (parts[2] + parts[1]) + parts[0])
         at += members
-    copies[3].wait()
+    copies[2].wait()
     for b in range(batches - 1):
         entries = mask_ref[b].astype(F32).astype(BF16)
         for later in range(b + 1, batches):
@@ -213,34 +210,33 @@
         return [ref.at[j, h].reshape(members * sub, lanes) for h in range(halves)]
 
     def update(levels):
-        every = list(range(len(levels)))
         src = [lines(state, j) for j, _ in levels]
         dst = [lines(result, j) for j, _ in levels]
         at = [pl.ds(level, members, stride=sub) for _, level in levels]
-        cells = [jnp.concatenate([r[at[k], :] for r in src[k]], axis=1) for k in every]
-
-        def first(b, k):
-            hi, low = split(cells[k])
-            sbuf[k, :members] = hi
-            sbuf[k, members:] = low
-            stack = jnp.concatenate([sbuf[k, :members], sbuf[k]], axis=0)
-            proj = mm(wide[b][:, : 3 * members], stack, precision=None)
-            hi, low = split(proj * open_mask[b])
-            pbuf[k, :count] = hi
-            pbuf[k, count:] = low
-
-        def second(b, k):
-            both = mm(coef[b], pbuf[k], precision=None)
-            cells[k] = cells[k] + (both[:members] + both[members:])
-
+        teams = [range(k, k + ABREAST) for k in range(0, len(levels), ABREAST)]
+        every = list(range(len(teams)))
+        cells = [
+            jnp.concatenate([r[at[k], :] for k in team for r in src[k]], axis=1) for team in teams
+        ]
         for b in range(batches):
             for k in every:
-                first(b, k)
+                hi, low = split(cells[k])
+                sbuf[k, :members] = hi
+                sbuf[k, members:] = low
+                stack = jnp.concatenate([sbuf[k, :members], sbuf[k]], axis=0)
+                proj = mm(wide[b][:, : 3 * members], stack, precision=None)
+                passed = jnp.concatenate([open_mask[b]] * ABREAST, axis=1)
+                hi, low = split(proj * passed)
+                pbuf[k, :count] = hi
+                pbuf[k, count:] = low
             for k in every:
-                second(b, k)
-        for k in every:
-            for h in range(halves):
-                dst[k][h][at[k], :] = cells[k][:, h * lanes : (h + 1) * lanes]
+                both = mm(coef[b], pbuf[k], precision=None)
+                cells[k] = cells[k] + (both[:members] + both[members:])
+        for k, team in enumerate(teams):
+            for i, level in enumerate(team):
+                for h in range(halves):
+                    cut = (i * halves + h) * lanes
+                    dst[level][h][at[level], :] = cells[k][:, cut : cut + lanes]
 
     def begin():
         return [rows_ref[b * members : (b + 1) * members, :] for b in range(batches)]
@@ -311,6 +307,8 @@
     batches, count = obs_block.shape
     n_lon = lax.axis_size("lon")
     n_lat = lax.axis_size("lat")
+    here = lax.axis_index("lon") * n_lat + lax.axis_index("lat")
+    key = jnp.where(obs_block == here, obs_column, -1)
     sub, lanes = 8, 128
     halves = columns // lanes
     chunks = levels // sub
@@ -324,21 +322,20 @@
     vmem = pl.BlockSpec(memory_space=pltpu.VMEM)
     hbm = pl.BlockSpec(memory_space=pltpu.HBM)
     packed = pl.pallas_call(
-        functools.partial(pick_kernel, n_lat, direct),
+        functools.partial(pick_kernel, direct),
         out_shape=[jax.ShapeDtypeStruct(shape, F32) for shape in shapes],
-        in_specs=[hbm, hbm, hbm, hbm],
+        in_specs=[hbm, hbm, hbm],
         out_specs=[vmem] * len(shapes),
         scratch_shapes=[
             pltpu.VMEM(packed_shape, F32),
             pltpu.VMEM((batches, count), jnp.int32),
-            pltpu.VMEM((batches, count), jnp.int32),
             pltpu.VMEM((batches - 1, count, columns), jnp.int32),
             pltpu.VMEM((members, columns), F32),
-            pltpu.SemaphoreType.DMA((4,)),
+            pltpu.SemaphoreType.DMA((3,)),
         ],
         compiler_params=pltpu.CompilerParams(vmem_limit_bytes=VMEM_LIMIT),
         name="pick",
-    )(obs_block, obs_column, masks, field)
+    )(key, masks, field)
     rows = exchange(packed)
     result = pl.pallas_call(
         functools.partial(assimilate_kernel, batches, members),
@@ -351,8 +348,8 @@
             pltpu.VMEM((batches, count, -(-3 * members // 128) * 128), BF16),
             pltpu.VMEM((batches, 2 * members, 2 * count), BF16),
             pltpu.VMEM((batches, count, columns), F32),
-            pltpu.VMEM((LEVELS_AT_ONCE, 2 * members, columns), BF16),
-            pltpu.VMEM((LEVELS_AT_ONCE, 2 * count, columns), BF16),
+            pltpu.VMEM((LEVELS_AT_ONCE // ABREAST, 2 * members, ABREAST * columns), BF16),
+            pltpu.VMEM((LEVELS_AT_ONCE // ABREAST, 2 * count, ABREAST * columns), BF16),
             pltpu.VMEM((batches, count, columns), jnp.int32),
             pltpu.SemaphoreType.DMA((chunks, halves)),
             pltpu.SemaphoreType.DMA((chunks, halves)),

time: 42.4 us -> 41.7 us (0.983)
  local copies, waits for them, and re-layouts: 1.4 us -> 0.01 us
  other arithmetic: 0.05 us -> 0.78 us
    unnamed x8 -> x4, local copies, waits for them, and re-layouts: 1.4 us -> 0.01 us
    select_n x0 -> x1, other arithmetic: none -> 0.73 us  [body(): key = jnp.where(obs_block == here, obs_column, -1)]
where the time goes in v4:
time: 41.7 us; the launch traced here: 41.5 us
  Pallas kernels  12.8 us (31%)
  starting transfers between devices  9.46 us (23%)
  blocking collectives  9.42 us (23%)
  waiting for transfers between devices  9.1 us (22%)
  other arithmetic  0.78 us (2%)
    pallas_call x1, Pallas kernels, body(): pl.pallas_call(functools.partial(assimilate_kernel, batches, members), ou...  11.3 us
    all_gather x1, blocking collectives, exchange(): return lax.all_gather(y, 'lon', axis=0, tiled=True)  9.42 us
    ppermute x3, starting transfers between devices, exchange(): lax.ppermute(y, 'lat', pairs)  4.45 us
    ppermute x3, starting transfers between devices, exchange(): lax.ppermute(y[k], 'lon', [(i, i ^ 2 * k) for i in range(n_lon)])  4.45 us
    ppermute x3, waiting for transfers between devices, exchange(): lax.ppermute(y, 'lat', pairs)  4.12 us
    ppermute x3, waiting for transfers between devices, exchange(): lax.ppermute(y[k], 'lon', [(i, i ^ 2 * k) for i in range(n_lon)])  3.95 us
    pallas_call x1, Pallas kernels, body(): pl.pallas_call(functools.partial(pick_kernel, direct), out_shape=[jax.Sha...  1.44 us
    ppermute x1, waiting for transfers between devices, exchange(): met = lax.ppermute(x[0], 'lon', [(i, i ^ 1) for i in range(n_lon)])  1.03 us
  transfers between devices with their start and end apart: 7, of which 6 were waited for; matrix products, arithmetic and copies ran while one was open for 0% of the time, Pallas kernels for 0%

profile of v4, /device:TPU:0, one launch (start us, length us, event | category | flops | bytes accessed | tf_op | source)
XLA Modules:
  0.0 41.5 jit_solution(4116979143824249145)
XLA Ops:
  0.0 0.0 copy-start.1
  0.0 0.0 copy-start
  0.0 0.7 %compare_select_fusion.key_hbm = s32[3,128]{1,0:T(4,128)S(1)} fusion(s32[3,128]{1,0:T(4,128)} %param.8, s32[3,128]{1,0:T(4,128)} %param.7, s32[]{:T(128)S(6)} %add.33), kind=kLoop, calls=%fused_computation.12 | loop fusion | flops 768 | bytes 4612 | tf_op jit(solution)/shard_map/jit(_where)/select_n | solution.py:311
  0.7 1.4 %pick.1 = (f32[4,80,128]{2,1,0:T(8,128)S(1)}, f32[80,128]{1,0:T(8,128)S(1)}, f32[80,128]{1,0:T(8,128)S(1)}, f32[80,128]{1,0:T(8,128)S(1)}, f32[80,128]{1,0:T(8,128)S(1)}) custom-call(s32[3,128]{1,0:T(4,128)S(1)} %compare_select_fusion.key_hbm, s32[3,128,256]{2,1,0:T(8,128)} %bitcast.28, f32[80,32,256]{2,1,0:T(8,128)} %bitcast.26), custom_call_target="tpu_custom_call" | custom-call | tf_op jit(solution)/shard_map/pick/pallas_call | solution.py:324
  2.2 0.6 %collective-permute-start = (f32[4,80,128]{2,1,0:T(8,128)S(1)}, f32[4,80,128]{2,1,0:T(8,128)S(1)}, u32[]{:S(2)}, u32[]{:S(2)}) collective-permute-start(f32[4,80,128]{2,1,0:T(8,128)S(1)} %get-tuple-element.11), channel_id=1, source_target_pairs={{0,4},{4,0},{8,12},{12,8},{16,20},{20,16},{24,28},{28,24},{1,5},{5... | collective-permute-start | bytes 491528 | tf_op jit(solution)/shard_map/ppermute | solution.py:280
  2.7 1.0 %collective-permute-done = f32[4,80,128]{2,1,0:T(8,128)S(1)} collective-permute-done((f32[4,80,128]{2,1,0:T(8,128)S(1)}, f32[4,80,128]{2,1,0:T(8,128)S(1)}, u32[]{:S(2)}, u32[]{:S(2)}) %collective-permute-start) | collective-permute-done | bytes 163872 | tf_op jit(solution)/shard_map/ppermute | solution.py:280
  3.8 2.9 %collective-permute-start.1 = (f32[80,128]{1,0:T(8,128)S(1)}, f32[80,128]{1,0:T(8,128)S(1)}, u32[]{:S(2)}, u32[]{:S(2)}) collective-permute-start(f32[80,128]{1,0:T(8,128)S(1)} %get-tuple-element.15), channel_id=1, source_target_pairs={{0,8},{4,12},{8,0},{12,4},{16,24},{20,28},{24,16},{28,20},{1,9},{5... | collective-permute-start | bytes 122888 | tf_op jit(solution)/shard_map/ppermute | solution.py:283
  6.7 1.5 %collective-permute-start.3 = (f32[80,128]{1,0:T(8,128)S(1)}, f32[80,128]{1,0:T(8,128)S(1)}, u32[]{:S(2)}, u32[]{:S(2)}) collective-permute-start(f32[80,128]{1,0:T(8,128)S(1)} %get-tuple-element.16), channel_id=1, source_target_pairs={{0,24},{4,28},{8,16},{12,20},{16,8},{20,12},{24,0},{28,4},{1,25},{... | collective-permute-start | bytes 122888 | tf_op jit(solution)/shard_map/ppermute | solution.py:283
  8.2 0.1 collective-permute-start.2
  8.2 0.4 %collective-permute-done.1 = f32[80,128]{1,0:T(8,128)S(1)} collective-permute-done((f32[80,128]{1,0:T(8,128)S(1)}, f32[80,128]{1,0:T(8,128)S(1)}, u32[]{:S(2)}, u32[]{:S(2)}) %collective-permute-start.1) | collective-permute-done | bytes 40992 | tf_op jit(solution)/shard_map/ppermute | solution.py:283
  8.7 2.9 %collective-permute-done.3 = f32[80,128]{1,0:T(8,128)S(1)} collective-permute-done((f32[80,128]{1,0:T(8,128)S(1)}, f32[80,128]{1,0:T(8,128)S(1)}, u32[]{:S(2)}, u32[]{:S(2)}) %collective-permute-start.3) | collective-permute-done | bytes 40992 | tf_op jit(solution)/shard_map/ppermute | solution.py:283
  11.6 0.6 %collective-permute-done.2 = f32[80,128]{1,0:T(8,128)S(1)} collective-permute-done((f32[80,128]{1,0:T(8,128)S(1)}, f32[80,128]{1,0:T(8,128)S(1)}, u32[]{:S(2)}, u32[]{:S(2)}) %collective-permute-start.2) | collective-permute-done | bytes 40992 | tf_op jit(solution)/shard_map/ppermute | solution.py:283
  12.2 3.7 %collective-permute-start.6 = (f32[80,128]{1,0:T(8,128)S(1)}, f32[80,128]{1,0:T(8,128)S(1)}, u32[]{:S(2)}, u32[]{:S(2)}) collective-permute-start(f32[80,128]{1,0:T(8,128)S(1)} %fusion.6), channel_id=1, source_target_pairs={{0,3},{1,2},{2,1},{3,0},{4,7},{5,6},{6,5},{7,4},{8,11},{9,10},{10,... | collective-permute-start | bytes 122888 | tf_op jit(solution)/shard_map/ppermute | solution.py:294
  15.9 0.0 collective-permute-start.5
  15.9 0.8 %collective-permute-start.4 = (f32[80,128]{1,0:T(8,128)S(1)}, f32[80,128]{1,0:T(8,128)S(1)}, u32[]{:S(2)}, u32[]{:S(2)}) collective-permute-start(f32[80,128]{1,0:T(8,128)S(1)} %fusion.6), channel_id=1, source_target_pairs={{0,1},{1,0},{2,3},{3,2},{4,5},{5,4},{6,7},{7,6},{8,9},{9,8},{10,11... | collective-permute-start | bytes 122888 | tf_op jit(solution)/shard_map/ppermute | solution.py:294
  16.7 1.4 %collective-permute-done.6 = f32[80,128]{1,0:T(8,128)S(1)} collective-permute-done((f32[80,128]{1,0:T(8,128)S(1)}, f32[80,128]{1,0:T(8,128)S(1)}, u32[]{:S(2)}, u32[]{:S(2)}) %collective-permute-start.6) | collective-permute-done | bytes 40992 | tf_op jit(solution)/shard_map/ppermute | solution.py:294
  18.1 2.7 %collective-permute-done.5 = f32[80,128]{1,0:T(8,128)S(1)} collective-permute-done((f32[80,128]{1,0:T(8,128)S(1)}, f32[80,128]{1,0:T(8,128)S(1)}, u32[]{:S(2)}, u32[]{:S(2)}) %collective-permute-start.5) | collective-permute-done | bytes 40992 | tf_op jit(solution)/shard_map/ppermute | solution.py:294
  20.8 0.0 collective-permute-done.4
  20.8 9.4 %all_gather.3.rows_ref = f32[640,128]{1,0:T(8,128)S(1)} all-gather(f32[80,128]{1,0:T(8,128)S(1)} %add_add_fusion), channel_id=1, replica_groups=mesh['lon'=8,'lat'=4] {'lon'}, dimensions={0}, use_global_device_ids=true | all-gather | bytes 368640 | tf_op jit(solution)/shard_map/all_gather | solution.py:302
  30.2 0.0 copy-done.1
  30.2 0.0 copy-done
  30.2 11.3 %assimilate.1 = f32[80,4,8,256]{3,2,1,0:T(8,128)} custom-call(f32[640,128]{1,0:T(8,128)S(1)} %all_gather.3.rows_ref, f32[3,128]{1,0:T(4,128)S(1)} %copy-done, f32[3,128]{1,0:T(4,128)S(1)} %copy-done.1, s32[3,128,256]{2,1,0:T(8,128)} %bitcast.29, f32[80,4,8,256]{3,2,1,0:T(8,128)} %bitcast.27), custom_call_target="tpu_custom_call" | custom-call | tf_op jit(solution)/shard_map/assimilate/pallas_call | solution.py:340
  (3 shorter events, 0.1 us)
Async XLA Ops:
  0.0 30.2 %copy-start.1 = (f32[3,128]{1,0:T(4,128)S(1)}, f32[3,128]{1,0:T(4,128)}, u32[]{:S(2)}) copy-start(f32[3,128]{1,0:T(4,128)} %error_ref.1) | copy-start | bytes 4612
  0.0 30.2 %copy-start = (f32[3,128]{1,0:T(4,128)S(1)}, f32[3,128]{1,0:T(4,128)}, u32[]{:S(2)}) copy-start(f32[3,128]{1,0:T(4,128)} %value_ref.1) | copy-start | bytes 4612
  2.2 1.6 %collective-permute-start = (f32[4,80,128]{2,1,0:T(8,128)S(1)}, f32[4,80,128]{2,1,0:T(8,128)S(1)}, u32[]{:S(2)}, u32[]{:S(2)}) collective-permute-start(f32[4,80,128]{2,1,0:T(8,128)S(1)} %get-tuple-element.11), channel_id=1, source_target_pairs={{0,4},{4,0},{8,12},{12,8},{16,20},{20,16},{24,28},{28,24},{1,5},{5... | collective-permute-start | bytes 491528 | tf_op jit(solution)/shard_map/ppermute | solution.py:280
  3.8 4.9 %collective-permute-start.1 = (f32[80,128]{1,0:T(8,128)S(1)}, f32[80,128]{1,0:T(8,128)S(1)}, u32[]{:S(2)}, u32[]{:S(2)}) collective-permute-start(f32[80,128]{1,0:T(8,128)S(1)} %get-tuple-element.15), channel_id=1, source_target_pairs={{0,8},{4,12},{8,0},{12,4},{16,24},{20,28},{24,16},{28,20},{1,9},{5... | collective-permute-start | bytes 122888 | tf_op jit(solution)/shard_map/ppermute | solution.py:283
  6.7 4.9 %collective-permute-start.3 = (f32[80,128]{1,0:T(8,128)S(1)}, f32[80,128]{1,0:T(8,128)S(1)}, u32[]{:S(2)}, u32[]{:S(2)}) collective-permute-start(f32[80,128]{1,0:T(8,128)S(1)} %get-tuple-element.16), channel_id=1, source_target_pairs={{0,24},{4,28},{8,16},{12,20},{16,8},{20,12},{24,0},{28,4},{1,25},{... | collective-permute-start | bytes 122888 | tf_op jit(solution)/shard_map/ppermute | solution.py:283
  8.2 4.0 %collective-permute-start.2 = (f32[80,128]{1,0:T(8,128)S(1)}, f32[80,128]{1,0:T(8,128)S(1)}, u32[]{:S(2)}, u32[]{:S(2)}) collective-permute-start(f32[80,128]{1,0:T(8,128)S(1)} %get-tuple-element.17), channel_id=1, source_target_pairs={{0,16},{4,20},{8,24},{12,28},{16,0},{20,4},{24,8},{28,12},{1,17},{... | collective-permute-start | bytes 122888 | tf_op jit(solution)/shard_map/ppermute | solution.py:283
  12.2 5.9 %collective-permute-start.6 = (f32[80,128]{1,0:T(8,128)S(1)}, f32[80,128]{1,0:T(8,128)S(1)}, u32[]{:S(2)}, u32[]{:S(2)}) collective-permute-start(f32[80,128]{1,0:T(8,128)S(1)} %fusion.6), channel_id=1, source_target_pairs={{0,3},{1,2},{2,1},{3,0},{4,7},{5,6},{6,5},{7,4},{8,11},{9,10},{10,... | collective-permute-start | bytes 122888 | tf_op jit(solution)/shard_map/ppermute | solution.py:294
  15.9 4.9 %collective-permute-start.5 = (f32[80,128]{1,0:T(8,128)S(1)}, f32[80,128]{1,0:T(8,128)S(1)}, u32[]{:S(2)}, u32[]{:S(2)}) collective-permute-start(f32[80,128]{1,0:T(8,128)S(1)} %fusion.6), channel_id=1, source_target_pairs={{0,2},{1,3},{2,0},{3,1},{4,6},{5,7},{6,4},{7,5},{8,10},{9,11},{10,... | collective-permute-start | bytes 122888 | tf_op jit(solution)/shard_map/ppermute | solution.py:294
  15.9 4.9 %collective-permute-start.4 = (f32[80,128]{1,0:T(8,128)S(1)}, f32[80,128]{1,0:T(8,128)S(1)}, u32[]{:S(2)}, u32[]{:S(2)}) collective-permute-start(f32[80,128]{1,0:T(8,128)S(1)} %fusion.6), channel_id=1, source_target_pairs={{0,1},{1,0},{2,3},{3,2},{4,5},{5,4},{6,7},{7,6},{8,9},{9,8},{10,11... | collective-permute-start | bytes 122888 | tf_op jit(solution)/shard_map/ppermute | solution.py:294

commit v5 on v4

--- a/solution.py
+++ b/solution.py
@@ -290,7 +290,8 @@
     if n_lat <= 4:
         ring = [[(i, (i + k) % n_lat) for i in range(n_lat)] for k in range(1, n_lat)]
         if n_lat & (n_lat - 1) == 0:
-            ring = [[(i, i ^ k) for i in range(n_lat)] for k in range(1, n_lat)]
+            order = [2, 1, 3][: n_lat - 1] if n_lat > 2 else [1]
+            ring = [[(i, i ^ k) for i in range(n_lat)] for k in order]
         y = functools.reduce(jnp.add, [lax.ppermute(y, "lat", pairs) for pairs in ring], y)
     elif n_lat & (n_lat - 1) == 0:
         k = 1

time: 41.7 us -> 41.7 us (level)
  transfers between devices with their start and end apart: 7 -> 7, of which waited for: 6 -> 7; matrix products, arithmetic and copies ran while one was open for 0% -> 0% of each run, Pallas kernels for 0% -> 0%
where the time goes in v5:
time: 41.7 us; the launch traced here: 41.5 us
  Pallas kernels  12.8 us (31%)
  starting transfers between devices  9.46 us (23%)
  blocking collectives  9.42 us (23%)
  waiting for transfers between devices  9.1 us (22%)
  other arithmetic  0.78 us (2%)
    pallas_call x1, Pallas kernels, body(): pl.pallas_call(functools.partial(assimilate_kernel, batches, members), ou...  11.3 us
    all_gather x1, blocking collectives, exchange(): return lax.all_gather(y, 'lon', axis=0, tiled=True)  9.42 us
    ppermute x3, starting transfers between devices, exchange(): lax.ppermute(y, 'lat', pairs)  4.45 us
    ppermute x3, starting transfers between devices, exchange(): lax.ppermute(y[k], 'lon', [(i, i ^ 2 * k) for i in range(n_lon)])  4.45 us
    ppermute x3, waiting for transfers between devices, exchange(): lax.ppermute(y, 'lat', pairs)  4.12 us
    ppermute x3, waiting for transfers between devices, exchange(): lax.ppermute(y[k], 'lon', [(i, i ^ 2 * k) for i in range(n_lon)])  3.95 us
    pallas_call x1, Pallas kernels, body(): pl.pallas_call(functools.partial(pick_kernel, direct), out_shape=[jax.Sha...  1.44 us
    ppermute x1, waiting for transfers between devices, exchange(): met = lax.ppermute(x[0], 'lon', [(i, i ^ 1) for i in range(n_lon)])  1.03 us
  transfers between devices with their start and end apart: 7, of which 7 were waited for; matrix products, arithmetic and copies ran while one was open for 0% of the time, Pallas kernels for 0%

profile of v5, /device:TPU:0, one launch (start us, length us, event | category | flops | bytes accessed | tf_op | source)
XLA Modules:
  0.0 41.5 jit_solution(9485873813033356104)
XLA Ops:
  0.0 0.0 copy-start.1
  0.0 0.0 copy-start
  0.0 0.7 %compare_select_fusion.key_hbm = s32[3,128]{1,0:T(4,128)S(1)} fusion(s32[3,128]{1,0:T(4,128)} %param.8, s32[3,128]{1,0:T(4,128)} %param.7, s32[]{:T(128)S(6)} %add.33), kind=kLoop, calls=%fused_computation.12 | loop fusion | flops 768 | bytes 4612 | tf_op jit(solution)/shard_map/jit(_where)/select_n | solution.py:312
  0.7 1.4 %pick.1 = (f32[4,80,128]{2,1,0:T(8,128)S(1)}, f32[80,128]{1,0:T(8,128)S(1)}, f32[80,128]{1,0:T(8,128)S(1)}, f32[80,128]{1,0:T(8,128)S(1)}, f32[80,128]{1,0:T(8,128)S(1)}) custom-call(s32[3,128]{1,0:T(4,128)S(1)} %compare_select_fusion.key_hbm, s32[3,128,256]{2,1,0:T(8,128)} %bitcast.28, f32[80,32,256]{2,1,0:T(8,128)} %bitcast.26), custom_call_target="tpu_custom_call" | custom-call | tf_op jit(solution)/shard_map/pick/pallas_call | solution.py:325
  2.2 0.6 %collective-permute-start = (f32[4,80,128]{2,1,0:T(8,128)S(1)}, f32[4,80,128]{2,1,0:T(8,128)S(1)}, u32[]{:S(2)}, u32[]{:S(2)}) collective-permute-start(f32[4,80,128]{2,1,0:T(8,128)S(1)} %get-tuple-element.11), channel_id=1, source_target_pairs={{0,4},{4,0},{8,12},{12,8},{16,20},{20,16},{24,28},{28,24},{1,5},{5... | collective-permute-start | bytes 491528 | tf_op jit(solution)/shard_map/ppermute | solution.py:280
  2.7 1.0 %collective-permute-done = f32[4,80,128]{2,1,0:T(8,128)S(1)} collective-permute-done((f32[4,80,128]{2,1,0:T(8,128)S(1)}, f32[4,80,128]{2,1,0:T(8,128)S(1)}, u32[]{:S(2)}, u32[]{:S(2)}) %collective-permute-start) | collective-permute-done | bytes 163872 | tf_op jit(solution)/shard_map/ppermute | solution.py:280
  3.8 2.9 %collective-permute-start.1 = (f32[80,128]{1,0:T(8,128)S(1)}, f32[80,128]{1,0:T(8,128)S(1)}, u32[]{:S(2)}, u32[]{:S(2)}) collective-permute-start(f32[80,128]{1,0:T(8,128)S(1)} %get-tuple-element.15), channel_id=1, source_target_pairs={{0,8},{4,12},{8,0},{12,4},{16,24},{20,28},{24,16},{28,20},{1,9},{5... | collective-permute-start | bytes 122888 | tf_op jit(solution)/shard_map/ppermute | solution.py:283
  6.7 1.5 %collective-permute-start.3 = (f32[80,128]{1,0:T(8,128)S(1)}, f32[80,128]{1,0:T(8,128)S(1)}, u32[]{:S(2)}, u32[]{:S(2)}) collective-permute-start(f32[80,128]{1,0:T(8,128)S(1)} %get-tuple-element.16), channel_id=1, source_target_pairs={{0,24},{4,28},{8,16},{12,20},{16,8},{20,12},{24,0},{28,4},{1,25},{... | collective-permute-start | bytes 122888 | tf_op jit(solution)/shard_map/ppermute | solution.py:283
  8.2 0.1 collective-permute-start.2
  8.2 0.4 %collective-permute-done.1 = f32[80,128]{1,0:T(8,128)S(1)} collective-permute-done((f32[80,128]{1,0:T(8,128)S(1)}, f32[80,128]{1,0:T(8,128)S(1)}, u32[]{:S(2)}, u32[]{:S(2)}) %collective-permute-start.1) | collective-permute-done | bytes 40992 | tf_op jit(solution)/shard_map/ppermute | solution.py:283
  8.7 2.9 %collective-permute-done.3 = f32[80,128]{1,0:T(8,128)S(1)} collective-permute-done((f32[80,128]{1,0:T(8,128)S(1)}, f32[80,128]{1,0:T(8,128)S(1)}, u32[]{:S(2)}, u32[]{:S(2)}) %collective-permute-start.3) | collective-permute-done | bytes 40992 | tf_op jit(solution)/shard_map/ppermute | solution.py:283
  11.6 0.6 %collective-permute-done.2 = f32[80,128]{1,0:T(8,128)S(1)} collective-permute-done((f32[80,128]{1,0:T(8,128)S(1)}, f32[80,128]{1,0:T(8,128)S(1)}, u32[]{:S(2)}, u32[]{:S(2)}) %collective-permute-start.2) | collective-permute-done | bytes 40992 | tf_op jit(solution)/shard_map/ppermute | solution.py:283
  12.2 3.7 %collective-permute-start.6 = (f32[80,128]{1,0:T(8,128)S(1)}, f32[80,128]{1,0:T(8,128)S(1)}, u32[]{:S(2)}, u32[]{:S(2)}) collective-permute-start(f32[80,128]{1,0:T(8,128)S(1)} %fusion.6), channel_id=1, source_target_pairs={{0,3},{1,2},{2,1},{3,0},{4,7},{5,6},{6,5},{7,4},{8,11},{9,10},{10,... | collective-permute-start | bytes 122888 | tf_op jit(solution)/shard_map/ppermute | solution.py:295
  15.9 0.0 collective-permute-start.5
  15.9 0.8 %collective-permute-start.4 = (f32[80,128]{1,0:T(8,128)S(1)}, f32[80,128]{1,0:T(8,128)S(1)}, u32[]{:S(2)}, u32[]{:S(2)}) collective-permute-start(f32[80,128]{1,0:T(8,128)S(1)} %fusion.6), channel_id=1, source_target_pairs={{0,2},{1,3},{2,0},{3,1},{4,6},{5,7},{6,4},{7,5},{8,10},{9,11},{10,... | collective-permute-start | bytes 122888 | tf_op jit(solution)/shard_map/ppermute | solution.py:295
  16.7 1.4 %collective-permute-done.6 = f32[80,128]{1,0:T(8,128)S(1)} collective-permute-done((f32[80,128]{1,0:T(8,128)S(1)}, f32[80,128]{1,0:T(8,128)S(1)}, u32[]{:S(2)}, u32[]{:S(2)}) %collective-permute-start.6) | collective-permute-done | bytes 40992 | tf_op jit(solution)/shard_map/ppermute | solution.py:295
  18.1 1.8 %collective-permute-done.5 = f32[80,128]{1,0:T(8,128)S(1)} collective-permute-done((f32[80,128]{1,0:T(8,128)S(1)}, f32[80,128]{1,0:T(8,128)S(1)}, u32[]{:S(2)}, u32[]{:S(2)}) %collective-permute-start.5) | collective-permute-done | bytes 40992 | tf_op jit(solution)/shard_map/ppermute | solution.py:295
  19.9 0.9 %collective-permute-done.4 = f32[80,128]{1,0:T(8,128)S(1)} collective-permute-done((f32[80,128]{1,0:T(8,128)S(1)}, f32[80,128]{1,0:T(8,128)S(1)}, u32[]{:S(2)}, u32[]{:S(2)}) %collective-permute-start.4) | collective-permute-done | bytes 40992 | tf_op jit(solution)/shard_map/ppermute | solution.py:295
  20.8 9.4 %all_gather.3.rows_ref = f32[640,128]{1,0:T(8,128)S(1)} all-gather(f32[80,128]{1,0:T(8,128)S(1)} %add_add_fusion), channel_id=1, replica_groups=mesh['lon'=8,'lat'=4] {'lon'}, dimensions={0}, use_global_device_ids=true | all-gather | bytes 368640 | tf_op jit(solution)/shard_map/all_gather | solution.py:303
  30.2 0.0 copy-done.1
  30.2 0.0 copy-done
  30.2 11.3 %assimilate.1 = f32[80,4,8,256]{3,2,1,0:T(8,128)} custom-call(f32[640,128]{1,0:T(8,128)S(1)} %all_gather.3.rows_ref, f32[3,128]{1,0:T(4,128)S(1)} %copy-done, f32[3,128]{1,0:T(4,128)S(1)} %copy-done.1, s32[3,128,256]{2,1,0:T(8,128)} %bitcast.29, f32[80,4,8,256]{3,2,1,0:T(8,128)} %bitcast.27), custom_call_target="tpu_custom_call" | custom-call | tf_op jit(solution)/shard_map/assimilate/pallas_call | solution.py:341
  (3 shorter events, 0.1 us)
Async XLA Ops:
  0.0 30.2 %copy-start.1 = (f32[3,128]{1,0:T(4,128)S(1)}, f32[3,128]{1,0:T(4,128)}, u32[]{:S(2)}) copy-start(f32[3,128]{1,0:T(4,128)} %error_ref.1) | copy-start | bytes 4612
  0.0 30.2 %copy-start = (f32[3,128]{1,0:T(4,128)S(1)}, f32[3,128]{1,0:T(4,128)}, u32[]{:S(2)}) copy-start(f32[3,128]{1,0:T(4,128)} %value_ref.1) | copy-start | bytes 4612
  2.2 1.6 %collective-permute-start = (f32[4,80,128]{2,1,0:T(8,128)S(1)}, f32[4,80,128]{2,1,0:T(8,128)S(1)}, u32[]{:S(2)}, u32[]{:S(2)}) collective-permute-start(f32[4,80,128]{2,1,0:T(8,128)S(1)} %get-tuple-element.11), channel_id=1, source_target_pairs={{0,4},{4,0},{8,12},{12,8},{16,20},{20,16},{24,28},{28,24},{1,5},{5... | collective-permute-start | bytes 491528 | tf_op jit(solution)/shard_map/ppermute | solution.py:280
  3.8 4.9 %collective-permute-start.1 = (f32[80,128]{1,0:T(8,128)S(1)}, f32[80,128]{1,0:T(8,128)S(1)}, u32[]{:S(2)}, u32[]{:S(2)}) collective-permute-start(f32[80,128]{1,0:T(8,128)S(1)} %get-tuple-element.15), channel_id=1, source_target_pairs={{0,8},{4,12},{8,0},{12,4},{16,24},{20,28},{24,16},{28,20},{1,9},{5... | collective-permute-start | bytes 122888 | tf_op jit(solution)/shard_map/ppermute | solution.py:283
  6.7 4.9 %collective-permute-start.3 = (f32[80,128]{1,0:T(8,128)S(1)}, f32[80,128]{1,0:T(8,128)S(1)}, u32[]{:S(2)}, u32[]{:S(2)}) collective-permute-start(f32[80,128]{1,0:T(8,128)S(1)} %get-tuple-element.16), channel_id=1, source_target_pairs={{0,24},{4,28},{8,16},{12,20},{16,8},{20,12},{24,0},{28,4},{1,25},{... | collective-permute-start | bytes 122888 | tf_op jit(solution)/shard_map/ppermute | solution.py:283
  8.2 4.0 %collective-permute-start.2 = (f32[80,128]{1,0:T(8,128)S(1)}, f32[80,128]{1,0:T(8,128)S(1)}, u32[]{:S(2)}, u32[]{:S(2)}) collective-permute-start(f32[80,128]{1,0:T(8,128)S(1)} %get-tuple-element.17), channel_id=1, source_target_pairs={{0,16},{4,20},{8,24},{12,28},{16,0},{20,4},{24,8},{28,12},{1,17},{... | collective-permute-start | bytes 122888 | tf_op jit(solution)/shard_map/ppermute | solution.py:283
  12.2 5.9 %collective-permute-start.6 = (f32[80,128]{1,0:T(8,128)S(1)}, f32[80,128]{1,0:T(8,128)S(1)}, u32[]{:S(2)}, u32[]{:S(2)}) collective-permute-start(f32[80,128]{1,0:T(8,128)S(1)} %fusion.6), channel_id=1, source_target_pairs={{0,3},{1,2},{2,1},{3,0},{4,7},{5,6},{6,5},{7,4},{8,11},{9,10},{10,... | collective-permute-start | bytes 122888 | tf_op jit(solution)/shard_map/ppermute | solution.py:295
  15.9 4.0 %collective-permute-start.5 = (f32[80,128]{1,0:T(8,128)S(1)}, f32[80,128]{1,0:T(8,128)S(1)}, u32[]{:S(2)}, u32[]{:S(2)}) collective-permute-start(f32[80,128]{1,0:T(8,128)S(1)} %fusion.6), channel_id=1, source_target_pairs={{0,1},{1,0},{2,3},{3,2},{4,5},{5,4},{6,7},{7,6},{8,9},{9,8},{10,11... | collective-permute-start | bytes 122888 | tf_op jit(solution)/shard_map/ppermute | solution.py:295
  15.9 4.9 %collective-permute-start.4 = (f32[80,128]{1,0:T(8,128)S(1)}, f32[80,128]{1,0:T(8,128)S(1)}, u32[]{:S(2)}, u32[]{:S(2)}) collective-permute-start(f32[80,128]{1,0:T(8,128)S(1)} %fusion.6), channel_id=1, source_target_pairs={{0,2},{1,3},{2,0},{3,1},{4,6},{5,7},{6,4},{7,5},{8,10},{9,11},{10,... | collective-permute-start | bytes 122888 | tf_op jit(solution)/shard_map/ppermute | solution.py:295
